TPU v7x, 256 devices: a whole 4x4x8 slice. The times are simulated.
256 devices in a mesh: gx: 8 (over y, core), gy: 32 (over x, z).
Axes of the slice: x: 4, y: 4, z: 8, core: 2. Of those that a mesh axis runs over, the one named last changes fastest.
Arguments:
- right_side: float32 [64, 512, 256], P('gx', 'gy'), may hold values from -8 to 8
- velocity: float32 [3, 64, 512, 256], P(None, 'gx', 'gy'), may hold values from 0.1 to 3
- deflation: bfloat16 [32, 64, 512, 256], P(None, 'gx', 'gy'), may hold values from -0.1875 to 0.1875
- inverse_rows: float32 [8192, 8192], P(('gx', 'gy')), may hold values from -0.0625 to 0.0625
Outputs:
- solution_field: float32 [64, 512, 256], P('gx', 'gy')
- residual: float32 [64, 512, 256], P('gx', 'gy')
All inputs are finite; a program needn't handle non-finite values.
Results may differ from a plain program's by a relative error of at most 0.005.
Values sent between devices are 32-bit elements; how exact they have to be, the bound alone decides.
A program may use at most 64 MiB of HBM per device.

v0:
```python
import jax
import jax.numpy as jnp
from jax import lax
from jax.sharding import PartitionSpec as P

KD = 32
DEPTH = 2
CHEB = 4


cheb_center = 1.0
cheb_radius = 0.9


def with_halo(block, sides, width):
    for axis, dim in sides:
        count = lax.axis_size(axis)
        forward = [(i, i + 1) for i in range(count - 1)]
        backward = [(target, source) for source, target in forward]
        low = lax.ppermute(
            lax.slice_in_dim(block, block.shape[dim] - width, None, axis=dim), axis, forward
        )
        high = lax.ppermute(lax.slice_in_dim(block, 0, width, axis=dim), axis, backward)
        block = jnp.concatenate([low, block, high], axis=dim)
    return block


def upwind(padded, velocity):
    centre = padded[1:-1, 1:-1, 1:-1]
    diagonal = 6.0 + velocity[0] + velocity[1] + velocity[2]
    beside = padded[2:, 1:-1, 1:-1] + (1.0 + velocity[0]) * padded[:-2, 1:-1, 1:-1]
    beside = beside + padded[1:-1, 2:, 1:-1] + (1.0 + velocity[1]) * padded[1:-1, :-2, 1:-1]
    beside = beside + padded[1:-1, 1:-1, 2:] + (1.0 + velocity[2]) * padded[1:-1, 1:-1, :-2]
    return diagonal * centre - beside


def box_apply(field, velocity):
    return upwind(jnp.pad(field, 1), velocity)


def chebyshev(source, velocity, inside):
    inverse_diag = 1.0 / (6.0 + velocity[0] + velocity[1] + velocity[2])
    sigma_ratio = cheb_center / cheb_radius
    rho_now = 1.0 / sigma_ratio
    update = inverse_diag * source / cheb_center * inside
    estimate = update
    remainder = source
    for sweep_index in range(CHEB - 1):
        remainder = remainder - box_apply(update, velocity)
        rho_next = 1.0 / (2.0 * sigma_ratio - rho_now)
        update = (
            rho_next * rho_now * update + 2.0 * rho_next / cheb_radius * inverse_diag * remainder
        ) * inside
        estimate = estimate + update
        rho_now = rho_next
    return estimate


def apply_global(field, velocity):
    padded = with_halo(field, (("gx", 0), ("gy", 1)), 1)
    padded = jnp.pad(padded, ((0, 0), (0, 0), (1, 1)))
    return upwind(padded, velocity)


def precondition(residual, velocity, wide_velocity, flat_vectors, inverse_rows, inside):
    size_x, size_y, size_z = residual.shape
    coarse = jnp.dot(
        flat_vectors, residual.astype(jnp.bfloat16).reshape(-1), preferred_element_type=jnp.float32
    )
    gathered = lax.all_gather(coarse, ("gx", "gy"), axis=0, tiled=True)
    solved = jnp.dot(inverse_rows, gathered, precision=lax.Precision.HIGHEST)
    solved = solved.astype(jnp.bfloat16)
    correction = jnp.dot(solved, flat_vectors, preferred_element_type=jnp.float32).reshape(
        size_x, size_y, size_z
    )
    remaining = residual - apply_global(correction, velocity)
    source = with_halo(remaining, (("gx", 0), ("gy", 1)), DEPTH)
    estimate = chebyshev(source, wide_velocity, inside)
    return correction + estimate[DEPTH : DEPTH + size_x, DEPTH : DEPTH + size_y]


def local(right_side, velocity, deflation, inverse_rows):
    size_x, size_y, size_z = right_side.shape
    wide_velocity = with_halo(velocity, (("gx", 1), ("gy", 2)), DEPTH)
    rows_x = lax.axis_index("gx") * size_x - DEPTH + lax.iota(jnp.int32, size_x + 2 * DEPTH)
    rows_y = lax.axis_index("gy") * size_y - DEPTH + lax.iota(jnp.int32, size_y + 2 * DEPTH)
    inside_x = ((rows_x >= 0) & (rows_x < size_x * lax.axis_size("gx"))).astype(jnp.float32)
    inside_y = ((rows_y >= 0) & (rows_y < size_y * lax.axis_size("gy"))).astype(jnp.float32)
    inside = inside_x[:, None, None] * inside_y[None, :, None]
    flat_vectors = deflation.reshape(KD, -1)
    rho_now = lax.psum(jnp.sum(right_side * right_side), ("gx", "gy"))
    search = precondition(right_side, velocity, wide_velocity, flat_vectors, inverse_rows, inside)
    image = apply_global(search, velocity)
    denominator = lax.psum(jnp.sum(right_side * image), ("gx", "gy"))
    alpha_step = rho_now / denominator
    middle = right_side - alpha_step * image
    smoothed = precondition(middle, velocity, wide_velocity, flat_vectors, inverse_rows, inside)
    turned = apply_global(smoothed, velocity)
    cross, square = lax.psum((jnp.sum(turned * middle), jnp.sum(turned * turned)), ("gx", "gy"))
    omega_step = cross / square
    solution_field = alpha_step * search + omega_step * smoothed
    return (solution_field, middle - omega_step * turned)


def solution(mesh):
    return jax.shard_map(
        local,
        mesh=mesh,
        in_specs=(
            P("gx", "gy", None),
            P(None, "gx", "gy", None),
            P(None, "gx", "gy", None),
            P(("gx", "gy"), None),
        ),
        out_specs=(P("gx", "gy", None), P("gx", "gy", None)),
        check_vma=False,
    )
```

profile of v0, /device:TPU:1, one launch (start us, length us, event | category | flops | bytes accessed | tf_op | source)
XLA Modules:
  0.0 445.5 jit_solution(6390966304339603937)
XLA Ops:
  0.7 1.1 convert_bitcast_fusion.1
  1.7 2.8 fusion.8
  4.8 81.3 %all-reduce.10 = f32[8192]{0:T(1024)} all-reduce(f32[8192]{0:T(1024)S(1)} %dynamic-update-slice), channel_id=1, replica_groups=mesh['gx'=8,'gy'=32] {'gx','gy'}, use_global_device_ids=true, to_apply=%add.10 | all-reduce | flops 8192 | bytes 65536
  86.1 1.2 copy.11
  87.3 0.9 fusion.5
  88.3 0.4 copy-done.1
  88.7 0.4 fusion.131
  89.1 1.9 collective-permute-start.5
  91.0 2.4 collective-permute-start.4
  93.5 3.2 collective-permute-start
  96.6 1.9 collective-permute-start.1
  98.7 1.3 collective-permute-start.6
  100.0 4.0 collective-permute-start.7
  104.2 0.6 collective-permute-done.7
  104.8 0.2 select_maximum_fusion.10
  105.2 4.8 %collective-permute-start.8 = (f32[2,16,256]{2,1,0:T(8,128)S(1)}, f32[2,16,256]{2,1,0:T(8,128)S(1)}, u32[]{:S(2)}, u32[]{:S(2)}) collective-permute-start(f32[2,16,256]{2,1,0:T(8,128)S(1)} %get-tuple-element.52), channel_id=1, source_target_pairs={{0,32},{32,64},{64,96},{96,128},{128,160},{160,192},{192,224},{1,3... | collective-permute-start | bytes 98312 | tf_op jit(solution)/shard_map/ppermute | solution.py:20
  110.0 1.9 collective-permute-start.9
  112.1 3.9 collective-permute-start.2
  116.0 1.3 collective-permute-start.3
  117.4 4.0 collective-permute-start.10
  121.4 1.3 collective-permute-start.11
  122.9 3.0 collective-permute-done.11
  126.0 0.4 add_multiply_fusion.3
  126.5 0.4 bitcast_multiply_fusion.3
  126.9 0.3 fusion.39
  127.3 1.9 collective-permute-start.12
  129.3 5.6 %collective-permute-start.13 = (f32[1,16,256]{2,1,0:T(8,128)S(1)}, f32[1,16,256]{2,1,0:T(8,128)S(1)}, u32[]{:S(2)}, u32[]{:S(2)}) collective-permute-start(f32[1,16,256]{2,1,0:T(8,128)S(1)} %get-tuple-element.50), channel_id=1, source_target_pairs={{0,32},{32,64},{64,96},{96,128},{128,160},{160,192},{192,224},{1,3... | collective-permute-start | bytes 49160 | tf_op jit(solution)/shard_map/ppermute | solution.py:20
  134.9 0.8 collective-permute-done.13
  135.8 1.3 collective-permute-start.14
  137.1 4.0 collective-permute-start.15
  141.1 0.8 collective-permute-done.15
  142.1 0.8 multiply_reduce_fusion.2
  142.8 87.5 %all-reduce.13 = (f32[]{:T(128)}, f32[]{:T(128)}) all-reduce(f32[]{:T(128)} %get-tuple-element.5, f32[]{:T(128)} %get-tuple-element.4), channel_id=1, replica_groups=mesh['gx'=8,'gy'=32] {'gx','gy'}, use_global_device_ids=true, to_apply=%region_1.0 | all-reduce | flops 2 | bytes 16 | tf_op jit(solution)/shard_map/psum | solution.py:91
  231.8 3.0 fusion.11
  235.0 73.9 %all-reduce.11 = f32[8192]{0:T(1024)S(1)} all-reduce(f32[8192]{0:T(1024)S(1)} %dynamic-update-slice.1), channel_id=1, replica_groups=mesh['gx'=8,'gy'=32] {'gx','gy'}, use_global_device_ids=true, to_apply=%add.11 | all-reduce | flops 8192 | bytes 65536
  308.9 0.9 fusion.7
  309.8 2.0 fusion.132
  311.8 2.9 collective-permute-start.17
  314.8 1.9 collective-permute-start.16
  316.8 3.1 collective-permute-done.16
  319.9 1.3 collective-permute-start.18
  321.2 4.0 collective-permute-start.19
  325.2 0.8 collective-permute-done.19
  326.0 0.2 select_maximum_fusion.4
  326.4 3.1 collective-permute-start.20
  329.4 1.9 collective-permute-start.21
  331.4 3.3 collective-permute-done.21
  334.7 3.9 collective-permute-start.22
  338.6 1.3 collective-permute-start.23
  339.9 3.3 collective-permute-done.23
  343.3 0.4 add_multiply_fusion.1
  343.7 0.4 bitcast_multiply_fusion
  344.2 0.3 fusion.67
  344.4 1.1 fusion.80
  345.5 1.9 collective-permute-start.24
  347.4 3.6 collective-permute-start.25
  351.1 0.8 collective-permute-done.25
  352.0 1.3 collective-permute-start.26
  353.3 4.0 collective-permute-start.27
  357.3 0.8 collective-permute-done.27
  358.0 0.2 select_maximum_fusion
  358.3 0.7 multiply_reduce_fusion
  359.0 84.4 %all-reduce.12 = (f32[]{:T(128)}, f32[]{:T(128)}) all-reduce(f32[]{:T(128)} %get-tuple-element.3, f32[]{:T(128)} %get-tuple-element.2), channel_id=1, replica_groups=mesh['gx'=8,'gy'=32] {'gx','gy'}, use_global_device_ids=true, to_apply=%region_5.6 | all-reduce | flops 2 | bytes 16 | tf_op jit(solution)/shard_map/psum | solution.py:99
  444.8 0.7 multiply_subtract_fusion
  (77 shorter events, 2.2 us)
Async XLA Ops:
  0.6 86.7 %copy-start = (f32[32,8192]{1,0:T(8,128)S(1)}, f32[32,8192]{1,0:T(8,128)}, u32[]{:S(2)}) copy-start(f32[32,8192]{1,0:T(8,128)} %param.7) | copy-start | bytes 3145732
  0.6 85.5 %copy-start.3 = (bf16[32,8,16,256]{3,2,1,0:T(8,128)(2,1)S(1)}, bf16[32,8,16,256]{3,2,1,0:T(8,128)(2,1)}, u32[]{:S(2)}) copy-start(bf16[32,8,16,256]{3,2,1,0:T(8,128)(2,1)} %param.6) | copy-start | bytes 6291460
  86.1 1.2 copy-start.6
  87.3 1.4 copy-start.1
  87.3 6.1 %copy-start.2 = (f32[3,8,16,256]{3,2,1,0:T(8,128)S(1)}, f32[3,8,16,256]{3,2,1,0:T(8,128)}, u32[]{:S(2)}) copy-start(f32[3,8,16,256]{3,2,1,0:T(8,128)} %param.5) | copy-start | bytes 1179652
  88.3 16.8 %copy-start.4 = (f32[8,16,256]{2,1,0:T(8,128)S(1)}, f32[8,16,256]{2,1,0:T(8,128)}, u32[]{:S(2)}) copy-start(f32[8,16,256]{2,1,0:T(8,128)} %param.4) | copy-start | bytes 393220
  89.1 9.6 %collective-permute-start.5 = (f32[1,16,256]{2,1,0:T(8,128)S(1)}, f32[1,16,256]{2,1,0:T(8,128)S(1)}, u32[]{:S(2)}, u32[]{:S(2)}) collective-permute-start(f32[1,16,256]{2,1,0:T(8,128)S(1)} %slice.464), channel_id=1, source_target_pairs={{0,32},{32,64},{64,96},{96,128},{128,160},{160,192},{192,224},{1,3... | collective-permute-start | bytes 49160 | tf_op jit(solution)/shard_map/ppermute | solution.py:20
  91.0 7.7 %collective-permute-start.4 = (f32[1,16,256]{2,1,0:T(8,128)S(1)}, f32[1,16,256]{2,1,0:T(8,128)S(1)}, u32[]{:S(2)}, u32[]{:S(2)}) collective-permute-start(f32[1,16,256]{2,1,0:T(8,128)S(1)} %slice.461), channel_id=1, source_target_pairs={{32,0},{64,32},{96,64},{128,96},{160,128},{192,160},{224,192},{33,... | collective-permute-start | bytes 49160 | tf_op jit(solution)/shard_map/ppermute | solution.py:23
  93.5 18.5 %collective-permute-start = (f32[3,2,16,256]{3,2,1,0:T(8,128)S(1)}, f32[3,2,16,256]{3,2,1,0:T(8,128)S(1)}, u32[]{:S(2)}, u32[]{:S(2)}) collective-permute-start(f32[3,2,16,256]{3,2,1,0:T(8,128)S(1)} %get-tuple-element.31), channel_id=1, source_target_pairs={{0,32},{32,64},{64,96},{96,128},{128,160},{160,192},{192,224},{1,3... | collective-permute-start | bytes 294920 | tf_op jit(solution)/shard_map/ppermute | solution.py:20
  96.6 15.4 %collective-permute-start.1 = (f32[3,2,16,256]{3,2,1,0:T(8,128)S(1)}, f32[3,2,16,256]{3,2,1,0:T(8,128)S(1)}, u32[]{:S(2)}, u32[]{:S(2)}) collective-permute-start(f32[3,2,16,256]{3,2,1,0:T(8,128)S(1)} %get-tuple-element.30), channel_id=1, source_target_pairs={{32,0},{64,32},{96,64},{128,96},{160,128},{192,160},{224,192},{33,... | collective-permute-start | bytes 294920 | tf_op jit(solution)/shard_map/ppermute | solution.py:23
  98.7 5.4 %collective-permute-start.6 = (f32[10,1,256]{2,1,0:T(1,128)S(1)}, f32[10,1,256]{2,1,0:T(1,128)S(1)}, u32[]{:S(2)}, u32[]{:S(2)}) collective-permute-start(f32[10,1,256]{2,1,0:T(1,128)S(1)} %get-tuple-element.43), channel_id=1, source_target_pairs={{1,0},{2,1},{3,2},{4,3},{5,4},{6,5},{7,6},{8,7},{9,8},{10,9},{11,1... | collective-permute-start | bytes 30728 | tf_op jit(solution)/shard_map/ppermute | solution.py:23
  100.0 4.8 %collective-permute-start.7 = (f32[10,1,256]{2,1,0:T(1,128)S(1)}, f32[10,1,256]{2,1,0:T(1,128)S(1)}, u32[]{:S(2)}, u32[]{:S(2)}) collective-permute-start(f32[10,1,256]{2,1,0:T(1,128)S(1)} %get-tuple-element.42), channel_id=1, source_target_pairs={{0,1},{1,2},{2,3},{3,4},{4,5},{5,6},{6,7},{7,8},{8,9},{9,10},{10,1... | collective-permute-start | bytes 30728 | tf_op jit(solution)/shard_map/ppermute | solution.py:20
  105.2 12.1 %collective-permute-start.8 = (f32[2,16,256]{2,1,0:T(8,128)S(1)}, f32[2,16,256]{2,1,0:T(8,128)S(1)}, u32[]{:S(2)}, u32[]{:S(2)}) collective-permute-start(f32[2,16,256]{2,1,0:T(8,128)S(1)} %get-tuple-element.52), channel_id=1, source_target_pairs={{0,32},{32,64},{64,96},{96,128},{128,160},{160,192},{192,224},{1,3... | collective-permute-start | bytes 98312 | tf_op jit(solution)/shard_map/ppermute | solution.py:20
  110.0 7.3 %collective-permute-start.9 = (f32[2,16,256]{2,1,0:T(8,128)S(1)}, f32[2,16,256]{2,1,0:T(8,128)S(1)}, u32[]{:S(2)}, u32[]{:S(2)}) collective-permute-start(f32[2,16,256]{2,1,0:T(8,128)S(1)} %get-tuple-element.53), channel_id=1, source_target_pairs={{32,0},{64,32},{96,64},{128,96},{160,128},{192,160},{224,192},{33,... | collective-permute-start | bytes 98312 | tf_op jit(solution)/shard_map/ppermute | solution.py:23
  112.1 10.6 %collective-permute-start.2 = (f32[3,12,2,256]{3,2,1,0:T(2,128)S(1)}, f32[3,12,2,256]{3,2,1,0:T(2,128)S(1)}, u32[]{:S(2)}, u32[]{:S(2)}) collective-permute-start(f32[3,12,2,256]{3,2,1,0:T(2,128)S(1)} %get-tuple-element.28), channel_id=1, source_target_pairs={{0,1},{1,2},{2,3},{3,4},{4,5},{5,6},{6,7},{7,8},{8,9},{9,10},{10,1... | collective-permute-start | bytes 221192 | tf_op jit(solution)/shard_map/ppermute | solution.py:20
  116.0 6.7 %collective-permute-start.3 = (f32[3,12,2,256]{3,2,1,0:T(2,128)S(1)}, f32[3,12,2,256]{3,2,1,0:T(2,128)S(1)}, u32[]{:S(2)}, u32[]{:S(2)}) collective-permute-start(f32[3,12,2,256]{3,2,1,0:T(2,128)S(1)} %get-tuple-element.29), channel_id=1, source_target_pairs={{1,0},{2,1},{3,2},{4,3},{5,4},{6,5},{7,6},{8,7},{9,8},{10,9},{11,1... | collective-permute-start | bytes 221192 | tf_op jit(solution)/shard_map/ppermute | solution.py:23
  117.4 5.5 %collective-permute-start.10 = (f32[12,2,256]{2,1,0:T(2,128)S(1)}, f32[12,2,256]{2,1,0:T(2,128)S(1)}, u32[]{:S(2)}, u32[]{:S(2)}) collective-permute-start(f32[12,2,256]{2,1,0:T(2,128)S(1)} %get-tuple-element.34), channel_id=1, source_target_pairs={{0,1},{1,2},{2,3},{3,4},{4,5},{5,6},{6,7},{7,8},{8,9},{9,10},{10,1... | collective-permute-start | bytes 73736 | tf_op jit(solution)/shard_map/ppermute | solution.py:20
  121.4 4.6 %collective-permute-start.11 = (f32[12,2,256]{2,1,0:T(2,128)S(1)}, f32[12,2,256]{2,1,0:T(2,128)S(1)}, u32[]{:S(2)}, u32[]{:S(2)}) collective-permute-start(f32[12,2,256]{2,1,0:T(2,128)S(1)} %get-tuple-element.35), channel_id=1, source_target_pairs={{1,0},{2,1},{3,2},{4,3},{5,4},{6,5},{7,6},{8,7},{9,8},{10,9},{11,1... | collective-permute-start | bytes 73736 | tf_op jit(solution)/shard_map/ppermute | solution.py:23
  122.9 4.3 copy-start.5
  127.3 7.6 %collective-permute-start.12 = (f32[1,16,256]{2,1,0:T(8,128)S(1)}, f32[1,16,256]{2,1,0:T(8,128)S(1)}, u32[]{:S(2)}, u32[]{:S(2)}) collective-permute-start(f32[1,16,256]{2,1,0:T(8,128)S(1)} %get-tuple-element.51), channel_id=1, source_target_pairs={{32,0},{64,32},{96,64},{128,96},{160,128},{192,160},{224,192},{33,... | collective-permute-start | bytes 49160 | tf_op jit(solution)/shard_map/ppermute | solution.py:23
  129.3 6.5 %collective-permute-start.13 = (f32[1,16,256]{2,1,0:T(8,128)S(1)}, f32[1,16,256]{2,1,0:T(8,128)S(1)}, u32[]{:S(2)}, u32[]{:S(2)}) collective-permute-start(f32[1,16,256]{2,1,0:T(8,128)S(1)} %get-tuple-element.50), channel_id=1, source_target_pairs={{0,32},{32,64},{64,96},{96,128},{128,160},{160,192},{192,224},{1,3... | collective-permute-start | bytes 49160 | tf_op jit(solution)/shard_map/ppermute | solution.py:20
  135.8 5.3 %collective-permute-start.14 = (f32[10,1,256]{2,1,0:T(1,128)S(1)}, f32[10,1,256]{2,1,0:T(1,128)S(1)}, u32[]{:S(2)}, u32[]{:S(2)}) collective-permute-start(f32[10,1,256]{2,1,0:T(1,128)S(1)} %get-tuple-element.41), channel_id=1, source_target_pairs={{1,0},{2,1},{3,2},{4,3},{5,4},{6,5},{7,6},{8,7},{9,8},{10,9},{11,1... | collective-permute-start | bytes 30728 | tf_op jit(solution)/shard_map/ppermute | solution.py:23
  137.1 4.8 %collective-permute-start.15 = (f32[10,1,256]{2,1,0:T(1,128)S(1)}, f32[10,1,256]{2,1,0:T(1,128)S(1)}, u32[]{:S(2)}, u32[]{:S(2)}) collective-permute-start(f32[10,1,256]{2,1,0:T(1,128)S(1)} %get-tuple-element.40), channel_id=1, source_target_pairs={{0,1},{1,2},{2,3},{3,4},{4,5},{5,6},{6,7},{7,8},{8,9},{9,10},{10,1... | collective-permute-start | bytes 30728 | tf_op jit(solution)/shard_map/ppermute | solution.py:20
  311.8 4.9 %collective-permute-start.17 = (f32[1,16,256]{2,1,0:T(8,128)S(1)}, f32[1,16,256]{2,1,0:T(8,128)S(1)}, u32[]{:S(2)}, u32[]{:S(2)}) collective-permute-start(f32[1,16,256]{2,1,0:T(8,128)S(1)} %slice.509), channel_id=1, source_target_pairs={{0,32},{32,64},{64,96},{96,128},{128,160},{160,192},{192,224},{1,3... | collective-permute-start | bytes 49160 | tf_op jit(solution)/shard_map/ppermute | solution.py:20
  314.8 5.1 %collective-permute-start.16 = (f32[1,16,256]{2,1,0:T(8,128)S(1)}, f32[1,16,256]{2,1,0:T(8,128)S(1)}, u32[]{:S(2)}, u32[]{:S(2)}) collective-permute-start(f32[1,16,256]{2,1,0:T(8,128)S(1)} %slice.506), channel_id=1, source_target_pairs={{32,0},{64,32},{96,64},{128,96},{160,128},{192,160},{224,192},{33,... | collective-permute-start | bytes 49160 | tf_op jit(solution)/shard_map/ppermute | solution.py:23
  319.9 5.3 %collective-permute-start.18 = (f32[10,1,256]{2,1,0:T(1,128)S(1)}, f32[10,1,256]{2,1,0:T(1,128)S(1)}, u32[]{:S(2)}, u32[]{:S(2)}) collective-permute-start(f32[10,1,256]{2,1,0:T(1,128)S(1)} %get-tuple-element.39), channel_id=1, source_target_pairs={{1,0},{2,1},{3,2},{4,3},{5,4},{6,5},{7,6},{8,7},{9,8},{10,9},{11,1... | collective-permute-start | bytes 30728 | tf_op jit(solution)/shard_map/ppermute | solution.py:23
  321.2 4.8 %collective-permute-start.19 = (f32[10,1,256]{2,1,0:T(1,128)S(1)}, f32[10,1,256]{2,1,0:T(1,128)S(1)}, u32[]{:S(2)}, u32[]{:S(2)}) collective-permute-start(f32[10,1,256]{2,1,0:T(1,128)S(1)} %get-tuple-element.38), channel_id=1, source_target_pairs={{0,1},{1,2},{2,3},{3,4},{4,5},{5,6},{6,7},{7,8},{8,9},{9,10},{10,1... | collective-permute-start | bytes 30728 | tf_op jit(solution)/shard_map/ppermute | solution.py:20
  326.4 5.0 %collective-permute-start.20 = (f32[2,16,256]{2,1,0:T(8,128)S(1)}, f32[2,16,256]{2,1,0:T(8,128)S(1)}, u32[]{:S(2)}, u32[]{:S(2)}) collective-permute-start(f32[2,16,256]{2,1,0:T(8,128)S(1)} %get-tuple-element.46), channel_id=1, source_target_pairs={{0,32},{32,64},{64,96},{96,128},{128,160},{160,192},{192,224},{1,3... | collective-permute-start | bytes 98312 | tf_op jit(solution)/shard_map/ppermute | solution.py:20
  329.4 5.2 %collective-permute-start.21 = (f32[2,16,256]{2,1,0:T(8,128)S(1)}, f32[2,16,256]{2,1,0:T(8,128)S(1)}, u32[]{:S(2)}, u32[]{:S(2)}) collective-permute-start(f32[2,16,256]{2,1,0:T(8,128)S(1)} %get-tuple-element.47), channel_id=1, source_target_pairs={{32,0},{64,32},{96,64},{128,96},{160,128},{192,160},{224,192},{33,... | collective-permute-start | bytes 98312 | tf_op jit(solution)/shard_map/ppermute | solution.py:23
  334.7 5.2 %collective-permute-start.22 = (f32[12,2,256]{2,1,0:T(2,128)S(1)}, f32[12,2,256]{2,1,0:T(2,128)S(1)}, u32[]{:S(2)}, u32[]{:S(2)}) collective-permute-start(f32[12,2,256]{2,1,0:T(2,128)S(1)} %get-tuple-element.32), channel_id=1, source_target_pairs={{0,1},{1,2},{2,3},{3,4},{4,5},{5,6},{6,7},{7,8},{8,9},{9,10},{10,1... | collective-permute-start | bytes 73736 | tf_op jit(solution)/shard_map/ppermute | solution.py:20
  338.6 4.6 %collective-permute-start.23 = (f32[12,2,256]{2,1,0:T(2,128)S(1)}, f32[12,2,256]{2,1,0:T(2,128)S(1)}, u32[]{:S(2)}, u32[]{:S(2)}) collective-permute-start(f32[12,2,256]{2,1,0:T(2,128)S(1)} %get-tuple-element.33), channel_id=1, source_target_pairs={{1,0},{2,1},{3,2},{4,3},{5,4},{6,5},{7,6},{8,7},{9,8},{10,9},{11,1... | collective-permute-start | bytes 73736 | tf_op jit(solution)/shard_map/ppermute | solution.py:23
  345.5 5.6 %collective-permute-start.24 = (f32[1,16,256]{2,1,0:T(8,128)S(1)}, f32[1,16,256]{2,1,0:T(8,128)S(1)}, u32[]{:S(2)}, u32[]{:S(2)}) collective-permute-start(f32[1,16,256]{2,1,0:T(8,128)S(1)} %get-tuple-element.45), channel_id=1, source_target_pairs={{32,0},{64,32},{96,64},{128,96},{160,128},{192,160},{224,192},{33,... | collective-permute-start | bytes 49160 | tf_op jit(solution)/shard_map/ppermute | solution.py:23
  347.4 4.5 %collective-permute-start.25 = (f32[1,16,256]{2,1,0:T(8,128)S(1)}, f32[1,16,256]{2,1,0:T(8,128)S(1)}, u32[]{:S(2)}, u32[]{:S(2)}) collective-permute-start(f32[1,16,256]{2,1,0:T(8,128)S(1)} %get-tuple-element.44), channel_id=1, source_target_pairs={{0,32},{32,64},{64,96},{96,128},{128,160},{160,192},{192,224},{1,3... | collective-permute-start | bytes 49160 | tf_op jit(solution)/shard_map/ppermute | solution.py:20
  352.0 5.3 %collective-permute-start.26 = (f32[10,1,256]{2,1,0:T(1,128)S(1)}, f32[10,1,256]{2,1,0:T(1,128)S(1)}, u32[]{:S(2)}, u32[]{:S(2)}) collective-permute-start(f32[10,1,256]{2,1,0:T(1,128)S(1)} %get-tuple-element.37), channel_id=1, source_target_pairs={{1,0},{2,1},{3,2},{4,3},{5,4},{6,5},{7,6},{8,7},{9,8},{10,9},{11,1... | collective-permute-start | bytes 30728 | tf_op jit(solution)/shard_map/ppermute | solution.py:23
  353.3 4.8 %collective-permute-start.27 = (f32[10,1,256]{2,1,0:T(1,128)S(1)}, f32[10,1,256]{2,1,0:T(1,128)S(1)}, u32[]{:S(2)}, u32[]{:S(2)}) collective-permute-start(f32[10,1,256]{2,1,0:T(1,128)S(1)} %get-tuple-element.36), channel_id=1, source_target_pairs={{0,1},{1,2},{2,3},{3,4},{4,5},{5,6},{6,7},{7,8},{8,9},{9,10},{10,1... | collective-permute-start | bytes 30728 | tf_op jit(solution)/shard_map/ppermute | solution.py:20
where the time goes:
time: 447 us; the launch traced here: 446 us
  blocking collectives  327 us (73%)
  starting transfers between devices  75.8 us (17%)
  waiting for transfers between devices  17.4 us (4%)
  matrix products  10 us (2%)
  other arithmetic  8.6 us (2%)
    unnamed x2, blocking collectives  155 us
    psum x1, blocking collectives, local(): rho_now = lax.psum(jnp.sum(right_side * right_side), ('gx', 'gy'))  87.5 us
    psum x1, blocking collectives, local(): lax.psum((jnp.sum(turned * middle), jnp.sum(turned * turned)), ('gx', 'gy'))  84.4 us
    ppermute x14, starting transfers between devices, with_halo(): lax.ppermute(lax.slice_in_dim(block, block.shape[dim] - width, None, axis...  52.8 us
    ppermute x14, starting transfers between devices, with_halo(): lax.ppermute(lax.slice_in_dim(block, 0, width, axis=dim), axis, backward)  23 us
    ppermute x14, waiting for transfers between devices, with_halo(): lax.ppermute(lax.slice_in_dim(block, 0, width, axis=dim), axis, backward)  12.7 us
  transfers between devices with their start and end apart: 28, of which 10 were waited for; matrix products, arithmetic and copies ran while one was open for 0% of the time, Pallas kernels for 0%

commit v1 on v0

v1 whole, which is shorter than its diff:
```python
import jax
import jax.numpy as jnp
from jax import lax
from jax.experimental import pallas as pl
from jax.experimental.pallas import tpu as pltpu
from jax.sharding import PartitionSpec as P

F32 = jnp.float32
BF16 = jnp.bfloat16
MESH = pl.DeviceIdType.MESH
SX, SY, NZ = 8, 16, 256
KD = 32
DEPTH = 2
CHEB = 4
ZG = 8
QUAD = 128 // KD
ROWS = 24
SIGMA = 1.0 / 0.9


def iota(shape, dim):
    return lax.broadcasted_iota(jnp.int32, shape, dim)


def padded(low, middle, high):
    gap = 4 - low.shape[0]
    parts = [low, middle, high]
    if gap:
        fill = jnp.zeros((gap, NZ), F32)
        parts = [fill] + parts + [fill]
    return jnp.concatenate(parts, axis=0)


def kernel(
    ngx, ngy,
    r_hbm, vel_hbm, defl_hbm, inv_hbm, sol_ref, res_ref,
    defl, inv, base, base_lo, base_hi, base_plo, base_phi,
    coef, q24, corr, corr_lo, corr_hi, corr_plo, corr_phi, ext, left, upd_a, upd_b, est,
    face, face_lo, face_hi, face_own, face_plo, face_phi,
    img, img_lo, img_hi, img_plo, img_phi, search, image, wfield, row_a, row_b,
    local_sem, ag_send, ag_recv, halo_send, halo_recv,
):
    gx = lax.axis_index("gx")
    gy = lax.axis_index("gy")
    xg = ngy // ZG
    zpos = lax.rem(gy, ZG)
    xpos = lax.div(gy, ZG)
    line = xpos * ZG
    group = ngx * xg
    seat = gx * xg + xpos
    east, west = lax.rem(gx + 1, ngx), lax.rem(gx + ngx - 1, ngx)
    north, south = lax.rem(gy + 1, ngy), lax.rem(gy + ngy - 1, ngy)
    barrier = pltpu.get_barrier_semaphore()

    def line_peer(step):
        return (gx, line + lax.rem(zpos + step, ZG))

    def group_peer(step):
        other = lax.rem(seat + step, group)
        return (lax.div(other, xg), lax.rem(other, xg) * ZG + zpos)

    def greet(device):
        pl.semaphore_signal(barrier, inc=1, device_id=device, device_id_type=MESH)

    @pl.loop(1, ZG)
    def _(step):
        greet(line_peer(step))

    @pl.loop(1, group)
    def _(step):
        greet(group_peer(step))

    around = [
        (east, gy), (west, gy), (gx, north), (gx, south),
        (east, north), (west, north), (east, south), (west, south),
    ]
    for device in around:
        greet(device)

    own = pl.ds(DEPTH, SX)
    loads = [
        pltpu.make_async_copy(r_hbm, base.at[3, own], local_sem.at[0]),
        pltpu.make_async_copy(defl_hbm, defl, local_sem.at[1]),
        pltpu.make_async_copy(vel_hbm, base.at[pl.ds(0, 3), own], local_sem.at[2]),
        pltpu.make_async_copy(inv_hbm, inv, local_sem.at[3]),
    ]
    for load in loads:
        load.start()

    has_w, has_e = gx > 0, gx < ngx - 1
    has_s, has_n = gy > 0, gy < ngy - 1

    def remote(src, dst, send, recv, device):
        return pltpu.make_async_remote_copy(
            src_ref=src, dst_ref=dst, send_sem=send, recv_sem=recv,
            device_id=device, device_id_type=MESH,
        )

    def line_send(turn, row):
        row_a[turn, zpos] = row

        @pl.loop(1, ZG)
        def _(step):
            remote(row_a.at[turn, zpos], row_a.at[turn, zpos], ag_send.at[turn, 0],
                   ag_recv.at[turn, 0], line_peer(step)).start()

    def line_wait(turn):
        view = row_a.at[turn, pl.ds(0, ZG - 1)]
        remote(view, view, ag_send.at[turn, 0], ag_recv.at[turn, 0], (east, gy)).wait_recv()

    def group_send(turn, rows):
        row_b[turn, seat] = rows

        @pl.loop(1, group)
        def _(step):
            remote(row_b.at[turn, seat], row_b.at[turn, seat], ag_send.at[turn, 1],
                   ag_recv.at[turn, 1], group_peer(step)).start()

    def group_wait(turn):
        view = row_b.at[turn, pl.ds(0, group - 1)]
        remote(view, view, ag_send.at[turn, 1], ag_recv.at[turn, 1], (east, gy)).wait_recv()

    def gather_finish(turn):
        view = row_a.at[turn, pl.ds(0, ZG - 1)]
        remote(view, view, ag_send.at[turn, 0], ag_recv.at[turn, 0], (east, gy)).wait_send()
        view = row_b.at[turn, pl.ds(0, group - 1)]
        remote(view, view, ag_send.at[turn, 1], ag_recv.at[turn, 1], (east, gy)).wait_send()

    def halo_start(turn, width, mid, low, high, plow, phigh, lead=()):
        def at(ref, start, size):
            return ref.at[lead + (pl.ds(start, size),)]

        def go(src, dst, kind, device):
            remote(src, dst, halo_send.at[turn, kind], halo_recv.at[turn, kind], device).start()

        w = width
        go(at(phigh, SX - w, w), at(low, 0, w), 1, (east, north))
        go(at(phigh, 0, w), at(low, w + SX, w), 1, (west, north))
        go(at(plow, SX - w, w), at(high, 0, w), 2, (east, south))
        go(at(plow, 0, w), at(high, w + SX, w), 2, (west, south))
        go(at(phigh, 0, SX), at(low, w, SX), 1, (gx, north))
        go(at(plow, 0, SX), at(high, w, SX), 2, (gx, south))
        go(at(mid, SX, w), at(mid, 0, w), 0, (east, gy))
        go(at(mid, w, w), at(mid, w + SX, w), 0, (west, gy))

    def halo_wait(turn, width, mid, low, high, lead=(), what="recv"):
        views = [mid.at[lead + (pl.ds(0, 2 * width),)], low, high]
        for kind, view in enumerate(views):
            copy = remote(view, view, halo_send.at[turn, kind], halo_recv.at[turn, kind], (east, gy))
            if what == "recv":
                copy.wait_recv()
            else:
                copy.wait_send()

    def face_start(turn):
        slot = turn - 3

        def go(src, dst, kind, device):
            remote(src, dst, halo_send.at[turn, kind], halo_recv.at[turn, kind], device).start()

        go(face_phi.at[slot], face_lo.at[slot], 1, (gx, north))
        go(face_plo.at[slot], face_hi.at[slot], 2, (gx, south))
        go(face_own.at[slot, 1], face.at[slot, 0], 0, (east, gy))
        go(face_own.at[slot, 0], face.at[slot, 1], 0, (west, gy))

    def face_wait(turn, what="recv"):
        slot = turn - 3
        for kind, view in enumerate([face.at[slot], face_lo.at[slot], face_hi.at[slot]]):
            copy = remote(view, view, halo_send.at[turn, kind], halo_recv.at[turn, kind], (east, gy))
            if what == "recv":
                copy.wait_recv()
            else:
                copy.wait_send()

    lane_end = iota((ROWS, NZ), 1) == NZ - 1

    def stencil(p, before, centre, after):
        beside = after + coef[1, p] * before
        beside = beside + pltpu.roll(centre, ROWS - 1, 0) + coef[2, p] * pltpu.roll(centre, 1, 0)
        ahead = jnp.where(lane_end, 0.0, pltpu.roll(centre, NZ - 1, 1))
        beside = beside + ahead + coef[3, p] * pltpu.roll(centre, 1, 1)
        return coef[0, p] * centre - beside

    def split(value):
        top = value.astype(BF16)
        rest = (value - top.astype(F32)).astype(BF16)
        return jnp.concatenate([top, rest], axis=0)

    def weights(half, x):
        return defl[pl.ds(half * 16, 16), x].reshape(256, NZ)

    def restrict(plane, exact):
        totals = [None, None]
        for x in range(SX):
            value = plane(x)
            lhs = split(value) if exact else value.astype(BF16)
            for half in range(2):
                part = lax.dot_general(
                    lhs, weights(half, x), (((1,), (1,)), ((), ())), preferred_element_type=F32
                )
                totals[half] = part if totals[half] is None else totals[half] + part
        packed = []
        for total in totals:
            same = lax.rem(iota(total.shape, 0), 16) == lax.rem(iota(total.shape, 1), 16)
            kept = jnp.where(same, total, 0.0)
            packed.append(jnp.sum(kept.reshape(-1, 8, 256), axis=0))
        packed = jnp.concatenate(packed, axis=1)
        high = packed.astype(BF16).astype(F32)
        rest = packed - high
        middle = rest.astype(BF16).astype(F32)
        low = rest - middle
        stack = jnp.concatenate([high, middle, low, jnp.zeros_like(low)], axis=0).astype(BF16)
        pick = lax.div(iota((2 * 256, 128), 0), 16) == lax.rem(iota((2 * 256, 128), 1), KD)
        row = jnp.dot(stack, pick.astype(F32).astype(BF16), preferred_element_type=F32)
        row = jnp.sum(row, axis=0, keepdims=True)
        mine = lax.div(iota((1, 128), 1), KD) == lax.rem(zpos, QUAD)
        return jnp.where(mine, row, 0.0)

    def quads(turn):
        rows = []
        for start in range(0, ZG, QUAD):
            total = row_a[turn, start]
            for k in range(1, QUAD):
                total = total + row_a[turn, start + k]
            rows.append(total)
        return jnp.concatenate(rows, axis=0) if len(rows) > 1 else rows[0]

    def solve(turn, exact):
        per = ZG // QUAD
        sums = [jnp.zeros((KD, 128), F32) for _ in range(4)]
        for j in range(group * per):
            value = row_b[turn, j // per, pl.ds(j % per, 1), :]
            sums[j % 4] = sums[j % 4] + inv[:, pl.ds(j * 128, 128)] * value
        total = (sums[0] + sums[1]) + (sums[2] + sums[3])
        solved = jnp.sum(total, axis=1, keepdims=True)
        spread = jnp.where(
            iota((KD, KD * 16), 0) == lax.div(iota((KD, KD * 16), 1), 16), solved, 0.0
        )
        spread = jnp.sum(spread, axis=0, keepdims=True)
        shape = (16, KD * 16)
        lhs = jnp.where(iota(shape, 0) == lax.rem(iota(shape, 1), 16), spread, 0.0)
        return split(lhs) if exact else lhs.astype(BF16)

    def prolong(lhs, exact):
        for x in range(SX):
            out = jnp.dot(lhs[:, :256], weights(0, x), preferred_element_type=F32)
            out = out + jnp.dot(lhs[:, 256:], weights(1, x), preferred_element_type=F32)
            if exact:
                out = out[:16] + out[16:]
            corr[0, 3 + x] = out
            corr_plo[0, x] = out[0:4]
            corr_phi[0, x] = out[12:16]

    def smooth(turn, out_ref):
        rows = iota((ROWS, NZ), 0)
        inner = (rows >= 4) & (rows < 20)
        keep_y = inner | ((rows < 4) & has_s) | ((rows >= 20) & has_n)

        @pl.loop(0, SX + 6)
        def _(p):
            plane = padded(corr_lo[turn, p], corr[turn, p], corr_hi[turn, p])
            keep = keep_y & ((p >= 3) | has_w) & ((p < SX + 3) | has_e)
            ext[p] = jnp.where(keep, plane, 0.0)

        rho = 1.0 / SIGMA

        @pl.loop(0, SX + 4)
        def _(p):
            rest = q24[p] - stencil(p, ext[p], ext[p + 1], ext[p + 2])
            left[p] = rest
            upd = coef[4, p] * rest
            upd_a[p + 1] = upd
            est[p] = upd

        now, nxt = upd_a, upd_b
        for sweep in range(CHEB - 1):
            rho_next = 1.0 / (2.0 * SIGMA - rho)
            first, second = rho_next * rho, 2.0 * rho_next / 0.9
            lo = sweep
            last = sweep == CHEB - 2

            @pl.loop(lo, SX + 4 - lo)
            def _(p):
                rest = left[p] - stencil(p, now[p], now[p + 1], now[p + 2])
                upd = first * now[p + 1] + second * (coef[4, p] * rest)
                if last:
                    out_ref[p - 1] = (est[p] + upd) + ext[p + 1]
                else:
                    left[p] = rest
                    nxt[p + 1] = upd
                    est[p] = est[p] + upd

            rho = rho_next
            now, nxt = nxt, now

    def face_pack(turn, src):
        slot = turn - 3
        face_own[slot, 0] = src[1, pl.ds(4, 16), :]
        face_own[slot, 1] = src[SX, pl.ds(4, 16), :]

        @pl.loop(0, SX)
        def _(x):
            face_plo[slot, x] = src[x + 1, pl.ds(4, 1), :]
            face_phi[slot, x] = src[x + 1, pl.ds(19, 1), :]

    def face_place(turn, dst):
        slot = turn - 3
        zero4 = jnp.zeros((4, NZ), F32)
        dst[0] = jnp.where(has_w, jnp.concatenate([zero4, face[slot, 0], zero4], axis=0), 0.0)
        dst[SX + 1] = jnp.where(has_e, jnp.concatenate([zero4, face[slot, 1], zero4], axis=0), 0.0)
        rows = iota((ROWS, NZ), 0)

        @pl.loop(0, SX)
        def _(x):
            low = jnp.broadcast_to(jnp.where(has_s, face_lo[slot, x], 0.0), (ROWS, NZ))
            high = jnp.broadcast_to(jnp.where(has_n, face_hi[slot, x], 0.0), (ROWS, NZ))
            value = dst[x + 1]
            dst[x + 1] = jnp.where(rows == 3, low, jnp.where(rows == 20, high, value))

    def q_assemble(low, mid, high):
        @pl.loop(0, SX + 4)
        def _(p):
            q24[p] = padded(low(p), mid(p), high(p))

    for ref in (upd_a, upd_b):
        ref[0] = jnp.zeros((ROWS, NZ), F32)
        ref[SX + 5] = jnp.zeros((ROWS, NZ), F32)

    loads[0].wait()
    loads[1].wait()
    row = restrict(lambda x: base[3, DEPTH + x], FIRST_EXACT)
    loads[2].wait()

    @pl.loop(0, SX)
    def _(x):
        for c in range(4):
            plane = base[c, DEPTH + x]
            base_plo[c, x] = plane[0:2]
            base_phi[c, x] = plane[14:16]

    greetings = (ZG - 1) + (group - 1) + len(around)
    pl.semaphore_wait(barrier, greetings)
    line_send(0, row)
    every = (slice(None),)
    halo_start(0, DEPTH, base, base_lo, base_hi, base_plo, base_phi, every)
    line_wait(0)
    group_send(0, quads(0))
    halo_wait(0, DEPTH, base, base_lo, base_hi, every)

    rows = iota((ROWS, NZ), 0)
    cols = iota((ROWS, NZ), 1)
    keep_y = ((rows >= 4) & (rows < 20)) | ((rows >= 2) & (rows < 4) & has_s)
    keep_y = keep_y | ((rows >= 20) & (rows < 22) & has_n)

    @pl.loop(0, SX + 4)
    def _(p):
        w0, w1, w2, r = [padded(base_lo[c, p], base[c, p], base_hi[c, p]) for c in range(4)]
        diagonal = 6.0 + w0 + w1 + w2
        keep = keep_y & ((p >= DEPTH) | has_w) & ((p < SX + DEPTH) | has_e)
        coef[0, p] = diagonal
        coef[1, p] = 1.0 + w0
        coef[2, p] = 1.0 + w1
        coef[3, p] = jnp.where(cols == 0, 0.0, 1.0 + w2)
        coef[4, p] = jnp.where(keep, 1.0 / diagonal, 0.0)
        q24[p] = r

    loads[3].wait()

    def whole_precondition(turn, out_ref, exact, fill_q):
        group_wait(turn)
        lhs = solve(turn, exact)
        prolong_into(turn, lhs, exact)
        halo_start(1 + turn, 3, corr.at[turn], corr_lo.at[turn], corr_hi.at[turn],
                   corr_plo.at[turn], corr_phi.at[turn])
        fill_q()
        halo_wait(1 + turn, 3, corr.at[turn], corr_lo.at[turn], corr_hi.at[turn])
        smooth(turn, out_ref)
        face_pack(3 + turn, out_ref)
        face_start(3 + turn)
        face_wait(3 + turn)
        face_place(3 + turn, out_ref)

    def prolong_into(turn, lhs, exact):
        for x in range(SX):
            out = jnp.dot(lhs[:, :256], weights(0, x), preferred_element_type=F32)
            out = out + jnp.dot(lhs[:, 256:], weights(1, x), preferred_element_type=F32)
            if exact:
                out = out[:16] + out[16:]
            corr[turn, 3 + x] = out
            corr_plo[turn, x] = out[0:4]
            corr_phi[turn, x] = out[12:16]

    whole_precondition(0, search, FIRST_EXACT, lambda: None)

    @pl.loop(0, SX)
    def _(x):
        value = stencil(x + DEPTH, search[x], search[x + 1], search[x + 2])
        image[x] = value
        inner = value[4:20]
        img[DEPTH + x] = inner
        img_plo[x] = inner[0:2]
        img_phi[x] = inner[14:16]

    row = restrict(lambda x: img[DEPTH + x], True)
    line_send(1, row)
    halo_start(5, DEPTH, img, img_lo, img_hi, img_plo, img_phi)
    line_wait(1)
    group_send(1, quads(1))
    halo_wait(5, DEPTH, img, img_lo, img_hi)
    q_assemble(lambda p: img_lo[p], lambda p: img[p], lambda p: img_hi[p])
    whole_precondition(1, wfield, True, lambda: None)

    zero = jnp.zeros((8, NZ), F32)

    def fold(value):
        return value[0:8] + value[8:16]

    def products(x, sums):
        v = stencil(x + DEPTH, wfield[x], wfield[x + 1], wfield[x + 2])
        left[x] = v
        v = v[4:20]
        i = img[DEPTH + x]
        r = base[3, DEPTH + x]
        pairs = [(r, r), (r, i), (i, i), (v, r), (v, i), (v, v)]
        return tuple(s + fold(a * b) for s, (a, b) in zip(sums, pairs))

    sums = lax.fori_loop(0, SX, products, (zero,) * 6)
    lanes = iota((1, 128), 1)
    row = jnp.zeros((1, 128), F32)
    for k, s in enumerate(sums):
        s = jnp.sum(s, axis=0, keepdims=True)
        s = jnp.sum(s, axis=1, keepdims=True)
        row = jnp.where(lanes == k, s, row)
    line_send(2, row)
    line_wait(2)
    total = row_a[2, 0]
    for k in range(1, ZG):
        total = total + row_a[2, k]
    per = ZG // QUAD
    group_send(2, jnp.concatenate([total] * per, axis=0) if per > 1 else total)
    group_wait(2)
    total = jnp.sum(row_b[2], axis=0)[0:1]
    rr, ri, ii, vr, vi, vv = [
        jnp.sum(jnp.where(lanes == k, total, 0.0), axis=1, keepdims=True) for k in range(6)
    ]
    alpha = rr / ri
    cross = (ri - alpha * ii) - alpha * (vr - alpha * vi)
    square = ii - alpha * (2.0 * vi - alpha * vv)
    omega = cross / square

    @pl.loop(0, SX)
    def _(x):
        s = search[x + 1]
        i = image[x]
        sol = alpha * s + omega * (s - alpha * wfield[x + 1])
        sol_ref[x] = sol[4:20]
        shift = (alpha * i + omega * (i - alpha * left[x]))[4:20]
        res_ref[x] = base[3, DEPTH + x] - shift

    for turn in range(3):
        gather_finish(turn)
    halo_wait(0, DEPTH, base, base_lo, base_hi, every, "send")
    for turn in range(2):
        halo_wait(1 + turn, 3, corr.at[turn], corr_lo.at[turn], corr_hi.at[turn], (), "send")
        face_wait(3 + turn, "send")
    halo_wait(5, DEPTH, img, img_lo, img_hi, (), "send")


FIRST_EXACT = False


def solution(mesh):
    ngx, ngy = mesh.shape["gx"], mesh.shape["gy"]
    group = ngx * (ngy // ZG)
    vm = pltpu.VMEM

    def local(right_side, velocity, deflation, inverse_rows):
        out = jax.ShapeDtypeStruct((SX, SY, NZ), F32)
        plane = (ROWS, NZ)
        scratch = [
            vm((KD, SX, SY, NZ), BF16),
            vm(inverse_rows.shape, F32),
            vm((4, SX + 4, SY, NZ), F32),
            vm((4, SX + 4, 2, NZ), F32),
            vm((4, SX + 4, 2, NZ), F32),
            vm((4, SX, 2, NZ), F32),
            vm((4, SX, 2, NZ), F32),
            vm((5, SX + 4) + plane, F32),
            vm((SX + 4,) + plane, F32),
            vm((2, SX + 6, SY, NZ), F32),
            vm((2, SX + 6, 4, NZ), F32),
            vm((2, SX + 6, 4, NZ), F32),
            vm((2, SX, 4, NZ), F32),
            vm((2, SX, 4, NZ), F32),
            vm((SX + 6,) + plane, F32),
            vm((SX + 4,) + plane, F32),
            vm((SX + 6,) + plane, F32),
            vm((SX + 6,) + plane, F32),
            vm((SX + 4,) + plane, F32),
            vm((2, 2, SY, NZ), F32),
            vm((2, SX, 1, NZ), F32),
            vm((2, SX, 1, NZ), F32),
            vm((2, 2, SY, NZ), F32),
            vm((2, SX, 1, NZ), F32),
            vm((2, SX, 1, NZ), F32),
            vm((SX + 4, SY, NZ), F32),
            vm((SX + 4, 2, NZ), F32),
            vm((SX + 4, 2, NZ), F32),
            vm((SX, 2, NZ), F32),
            vm((SX, 2, NZ), F32),
            vm((SX + 2,) + plane, F32),
            vm((SX,) + plane, F32),
            vm((SX + 2,) + plane, F32),
            vm((3, ZG, 1, 128), F32),
            vm((3, group, ZG // QUAD, 128), F32),
            pltpu.SemaphoreType.DMA((4,)),
            pltpu.SemaphoreType.DMA((3, 2)),
            pltpu.SemaphoreType.DMA((3, 2)),
            pltpu.SemaphoreType.DMA((6, 3)),
            pltpu.SemaphoreType.DMA((6, 3)),
        ]

        def body(*refs):
            kernel(ngx, ngy, *refs)

        return pl.pallas_call(
            body,
            name="bicgstab",
            out_shape=(out, out),
            in_specs=[pl.BlockSpec(memory_space=pl.ANY)] * 4,
            out_specs=(pl.BlockSpec(memory_space=vm), pl.BlockSpec(memory_space=vm)),
            scratch_shapes=scratch,
            compiler_params=pltpu.CompilerParams(collective_id=0, has_side_effects=True),
        )(right_side, velocity, deflation, inverse_rows)

    return jax.shard_map(
        local,
        mesh=mesh,
        in_specs=(
            P("gx", "gy", None),
            P(None, "gx", "gy", None),
            P(None, "gx", "gy", None),
            P(("gx", "gy"), None),
        ),
        out_specs=(P("gx", "gy", None), P("gx", "gy", None)),
        check_vma=False,
    )
```

time: 447 us -> 72.4 us (0.16)
  blocking collectives: 327 us -> 0 us
  starting transfers between devices: 75.8 us -> 0 us
  Pallas kernels: 0 us -> 68.5 us
  waiting for transfers between devices: 17.4 us -> 0 us
  matrix products: 10 us -> 0 us
  other arithmetic: 8.6 us -> 0 us
    psum x2 -> x0, blocking collectives: 172 us -> none  [the longest x1 87.5 us: local(): rho_now = lax.psum(jnp.sum(right_side * right_side), ('gx', 'gy'))]
    unnamed x2 -> x0, blocking collectives: 155 us -> none
    ppermute x28 -> x0, starting transfers between devices: 75.8 us -> none  [the longest x14 52.8 us: with_halo(): lax.ppermute(lax.slice_in_dim(block, block.shape[dim] - width, None, axis...]
    pallas_call x0 -> x1, Pallas kernels: none -> 68.5 us  [local(): pl.pallas_call(body, name='bicgstab', out_shape=(out, out), in_specs=[pl....]
    ppermute x28 -> x0, waiting for transfers between devices: 17.4 us -> none  [the longest x14 12.7 us: with_halo(): lax.ppermute(lax.slice_in_dim(block, 0, width, axis=dim), axis, backward)]
    dot_general x6 -> x0, matrix products: 10 us -> none  [the longest x2 5.83 us: precondition(): jnp.dot(flat_vectors, residual.astype(jnp.bfloat16).reshape(-1), preferre...]
  transfers between devices with their start and end apart: 28 -> 0, of which waited for: 10 -> 0; matrix products, arithmetic and copies ran while one was open for 0% -> 0% of each run, Pallas kernels for 0% -> 0%
where the time goes in v1:
time: 72.4 us; the launch traced here: 72.3 us
  Pallas kernels  68.5 us (95%)
  local copies, waits for them, and re-layouts  3.14 us (4%)
    pallas_call x1, Pallas kernels, local(): pl.pallas_call(body, name='bicgstab', out_shape=(out, out), in_specs=[pl....  68.5 us
    unnamed x2, local copies, waits for them, and re-layouts  3.14 us

profile of v1, /device:TPU:1, one launch (start us, length us, event | category | flops | bytes accessed | tf_op | source)
XLA Modules:
  0.0 72.3 jit_solution(13291972479319498750)
XLA Ops:
  0.6 68.5 %bicgstab.1 = (f32[8,16,256]{2,1,0:T(8,128)}, f32[8,16,256]{2,1,0:T(8,128)}) custom-call(f32[8,16,256]{2,1,0:T(8,128)} %refs_0_.1, f32[3,8,16,256]{3,2,1,0:T(8,128)} %refs_1_.1, bf16[32,8,16,256]{3,2,1,0:T(8,128)(2,1)} %refs_2_.1, f32[32,8192]{1,0:T(8,128)} %refs_3_.1), custom_call_target="tpu_custom_call" | custom-call | tf_op jit(solution)/shard_map/bicgstab/pallas_call | solution.py:526
  69.2 1.6 %copy.8 = f32[8,16,256]{2,1,0:T(8,128)} copy(f32[8,16,256]{2,1,0:T(8,128)} %get-tuple-element.4) | data formatting | bytes 262144
  70.7 1.6 %copy.9 = f32[8,16,256]{2,1,0:T(8,128)} copy(f32[8,16,256]{2,1,0:T(8,128)} %get-tuple-element.5) | data formatting | bytes 262144

commit v2 on v1

v2 whole, which is shorter than its diff:
```python
import jax
import jax.numpy as jnp
from jax import lax
from jax.experimental import pallas as pl
from jax.experimental.pallas import tpu as pltpu
from jax.sharding import PartitionSpec as P

F32 = jnp.float32
BF16 = jnp.bfloat16
MESH = pl.DeviceIdType.MESH
SX, SY, NZ = 8, 16, 256
KD = 32
DEPTH = 2
CHEB = 4
ZG = 8
QUAD = 128 // KD
ROWS = 24
SIGMA = 1.0 / 0.9
AROUND = [(1, 1), (-1, 1), (1, -1), (-1, -1), (0, 1), (0, -1), (1, 0), (-1, 0)]


def iota(shape, dim):
    return lax.broadcasted_iota(jnp.int32, shape, dim)


def padded(low, middle, high):
    gap = 4 - low.shape[0]
    parts = [low, middle, high]
    if gap:
        fill = jnp.zeros((gap, NZ), F32)
        parts = [fill] + parts + [fill]
    return jnp.concatenate(parts, axis=0)


def kernel(
    ngx, ngy,
    r_hbm, vel_hbm, defl_hbm, inv_hbm, s_ref, i_ref, w_ref, v_ref, alpha_ref, omega_ref,
    defl, inv, base, base_lo, base_hi, base_plo, base_phi,
    coef, scale, pick, q24, corr, corr_lo, corr_hi, corr_plo, corr_phi, ext, left, upd0, upd1, upd2,
    face, face_lo, face_hi, face_own, face_plo, face_phi,
    img, img_lo, img_hi, img_plo, img_phi, search, wfield, row_a, row_b,
    local_sem, ag_send, ag_recv, halo_send, halo_recv,
):
    gx = lax.axis_index("gx")
    gy = lax.axis_index("gy")
    xg = ngy // ZG
    zpos = lax.rem(gy, ZG)
    xpos = lax.div(gy, ZG)
    line = xpos * ZG
    group = ngx * xg
    seat = gx * xg + xpos
    here = (gx, gy)
    barrier = pltpu.get_barrier_semaphore()

    def line_peer(step):
        return (gx, line + lax.rem(zpos + step, ZG))

    def group_peer(step):
        other = lax.rem(seat + step, group)
        return (lax.div(other, xg), lax.rem(other, xg) * ZG + zpos)

    def greet(device):
        pl.semaphore_signal(barrier, inc=1, device_id=device, device_id_type=MESH)

    own = pl.ds(DEPTH, SX)
    loads = [
        pltpu.make_async_copy(r_hbm, base.at[3, own], local_sem.at[0]),
        pltpu.make_async_copy(defl_hbm.at[pl.ds(0, 16)], defl.at[pl.ds(0, 16)], local_sem.at[1]),
        pltpu.make_async_copy(defl_hbm.at[pl.ds(16, 16)], defl.at[pl.ds(16, 16)], local_sem.at[2]),
        pltpu.make_async_copy(vel_hbm, base.at[pl.ds(0, 3), own], local_sem.at[3]),
        pltpu.make_async_copy(inv_hbm, inv, local_sem.at[4]),
    ]
    for load in loads:
        load.start()

    @pl.loop(1, ZG)
    def _(step):
        greet(line_peer(step))

    @pl.loop(1, group)
    def _(step):
        greet(group_peer(step))

    for dx, dy in AROUND:
        greet((lax.rem(gx + dx + ngx, ngx), lax.rem(gy + dy + ngy, ngy)))

    has_w, has_e = gx > 0, gx < ngx - 1
    has_s, has_n = gy > 0, gy < ngy - 1

    def remote(src, dst, send, recv, device):
        return pltpu.make_async_remote_copy(
            src_ref=src, dst_ref=dst, send_sem=send, recv_sem=recv,
            device_id=device, device_id_type=MESH,
        )

    def line_send(turn, row):
        row_a[turn, zpos] = row

        @pl.loop(1, ZG)
        def _(step):
            remote(row_a.at[turn, zpos], row_a.at[turn, zpos], ag_send.at[turn, 0],
                   ag_recv.at[turn, 0], line_peer(step)).start()

    def line_wait(turn):
        view = row_a.at[turn, pl.ds(0, ZG - 1)]
        remote(view, view, ag_send.at[turn, 0], ag_recv.at[turn, 0], here).wait_recv()

    def group_send(turn, rows):
        row_b[turn, seat] = rows

        @pl.loop(1, group)
        def _(step):
            remote(row_b.at[turn, seat], row_b.at[turn, seat], ag_send.at[turn, 1],
                   ag_recv.at[turn, 1], group_peer(step)).start()

    def group_wait(turn):
        view = row_b.at[turn, pl.ds(0, group - 1)]
        remote(view, view, ag_send.at[turn, 1], ag_recv.at[turn, 1], here).wait_recv()

    def gather_finish(turn):
        view = row_a.at[turn, pl.ds(0, ZG - 1)]
        remote(view, view, ag_send.at[turn, 0], ag_recv.at[turn, 0], here).wait_send()
        view = row_b.at[turn, pl.ds(0, group - 1)]
        remote(view, view, ag_send.at[turn, 1], ag_recv.at[turn, 1], here).wait_send()

    def beside(dx, dy):
        tests = {(-1, 0): has_w, (1, 0): has_e, (0, -1): has_s, (0, 1): has_n}
        first = tests.get((dx, 0)) if dx else None
        second = tests.get((0, dy)) if dy else None
        if first is None:
            return second
        return first if second is None else first & second

    def halo(what, turn, width, mid, low, high, plow, phigh, lead=()):
        w = width
        for k, (dx, dy) in enumerate(AROUND):
            size = w if dx else SX
            take = {1: SX - w, -1: 0, 0: 0}[dx]
            put = {1: 0, -1: w + SX, 0: w}[dx]
            source = {1: phigh, -1: plow, 0: mid}[dy]
            target = {1: low, -1: high, 0: mid}[dy]
            src = source.at[lead + (pl.ds(take + (0 if dy else w), size),)]
            dst = target.at[lead + (pl.ds(put, size),)]
            copy = remote(
                src, dst, halo_send.at[turn, k], halo_recv.at[turn, k],
                (gx + dx, gy + dy) if what == "start" else here,
            )
            act(what, copy, dx, dy)

    def act(what, copy, dx, dy):
        sign = -1 if what == "recv" else 1

        @pl.when(beside(sign * dx, sign * dy))
        def _():
            if what == "start":
                copy.start()
            elif what == "recv":
                copy.wait_recv()
            else:
                copy.wait_send()

    def faces(what, slot):
        pairs = [
            ((1, 0), face_own.at[slot, 1], face.at[slot, 0]),
            ((-1, 0), face_own.at[slot, 0], face.at[slot, 1]),
            ((0, 1), face_phi.at[slot], face_lo.at[slot]),
            ((0, -1), face_plo.at[slot], face_hi.at[slot]),
        ]
        for k, ((dx, dy), src, dst) in enumerate(pairs):
            copy = remote(
                src, dst, halo_send.at[4 + slot, k], halo_recv.at[4 + slot, k],
                (gx + dx, gy + dy) if what == "start" else here,
            )
            act(what, copy, dx, dy)

    lane_end = iota((ROWS, NZ), 1) == NZ - 1

    def shifts(before, centre, after, add, c0, c1, c2):
        ahead = jnp.where(lane_end, 0.0, pltpu.roll(centre, NZ - 1, 1))
        nexts = (after + pltpu.roll(centre, ROWS - 1, 0)) + ahead
        if add is not None:
            nexts = nexts + add
        previous = c0 * before + c1 * pltpu.roll(centre, 1, 0)
        return nexts, previous + c2 * pltpu.roll(centre, 1, 1)

    def operator(x, field):
        nexts, previous = shifts(
            field[x], field[x + 1], field[x + 2], None, coef[1, x], coef[2, x], coef[3, x]
        )
        return coef[0, x] * field[x + 1] - (nexts + previous)

    def split(value):
        top = value.astype(BF16)
        rest = (value - top.astype(F32)).astype(BF16)
        return jnp.concatenate([top, rest], axis=0)

    def weights(half, x):
        return defl[pl.ds(half * 16, 16), x].reshape(256, NZ)

    def restrict(plane, exact, ready=(None, None)):
        lhs = [split(plane(x)) if exact else plane(x).astype(BF16) for x in range(SX)]
        packed = []
        for half in range(2):
            if ready[half] is not None:
                ready[half].wait()
            total = None
            for x in range(SX):
                part = lax.dot_general(
                    lhs[x], weights(half, x), (((1,), (1,)), ((), ())), preferred_element_type=F32
                )
                total = part if total is None else total + part
            same = lax.rem(iota(total.shape, 0), 16) == lax.rem(iota(total.shape, 1), 16)
            kept = jnp.where(same, total, 0.0)
            packed.append(jnp.sum(kept.reshape(-1, 8, 256), axis=0))
        packed = jnp.concatenate(packed, axis=1)
        high = packed.astype(BF16).astype(F32)
        rest = packed - high
        middle = rest.astype(BF16).astype(F32)
        low = rest - middle
        stack = jnp.concatenate([high, middle, low, jnp.zeros_like(low)], axis=0).astype(BF16)
        row = jnp.dot(stack, pick[...], preferred_element_type=F32)
        row = jnp.sum(row, axis=0, keepdims=True)
        mine = lax.div(iota((1, 128), 1), KD) == lax.rem(zpos, QUAD)
        return jnp.where(mine, row, 0.0)

    def quads(turn):
        rows = []
        for start in range(0, ZG, QUAD):
            total = row_a[turn, start]
            for k in range(1, QUAD):
                total = total + row_a[turn, start + k]
            rows.append(total)
        return jnp.concatenate(rows, axis=0) if len(rows) > 1 else rows[0]

    def solve(turn, exact):
        per = ZG // QUAD
        sums = [jnp.zeros((KD, 128), F32) for _ in range(4)]
        for j in range(group * per):
            value = row_b[turn, j // per, pl.ds(j % per, 1), :]
            sums[j % 4] = sums[j % 4] + inv[:, pl.ds(j * 128, 128)] * value
        total = (sums[0] + sums[1]) + (sums[2] + sums[3])
        solved = jnp.sum(total, axis=1, keepdims=True)
        spread = jnp.where(
            iota((KD, KD * 16), 0) == lax.div(iota((KD, KD * 16), 1), 16), solved, 0.0
        )
        spread = jnp.sum(spread, axis=0, keepdims=True)
        shape = (16, KD * 16)
        lhs = jnp.where(iota(shape, 0) == lax.rem(iota(shape, 1), 16), spread, 0.0)
        return split(lhs) if exact else lhs.astype(BF16)

    def smooth(turn, out_ref, own_ref):
        rows = iota((ROWS, NZ), 0)
        keep_y = ((rows >= 4) & (rows < 20)) | ((rows < 4) & has_s) | ((rows >= 20) & has_n)
        box = (rows >= 2) & (rows < 22)

        @pl.loop(0, SX + 6, unroll=2)
        def _(p):
            plane = padded(corr_lo[turn, p], corr[turn, p], corr_hi[turn, p])
            keep = keep_y & ((p >= 3) | has_w) & ((p < SX + 3) | has_e)
            ext[p] = jnp.where(keep, plane, 0.0)

        def scaled(p, before, centre, after, add):
            nexts, previous = shifts(before, centre, after, add, scale[1, p], scale[2, p], scale[3, p])
            return scale[0, p] * nexts + previous

        @pl.loop(0, SX + 4, unroll=4)
        def _(p):
            centre = ext[p + 1]
            total = scaled(p, ext[p], centre, ext[p + 2], q24[p])
            upd0[p + 1] = total - jnp.where(box, centre, 0.0)

        rho = 1.0 / SIGMA
        factors = []
        for sweep in range(CHEB - 1):
            rho_next = 1.0 / (2.0 * SIGMA - rho)
            factors.append((rho_next * rho, 2.0 * rho_next / 0.9))
            rho = rho_next

        @pl.loop(0, SX + 4, unroll=4)
        def _(p):
            centre = upd0[p + 1]
            rest = scaled(p, upd0[p], centre, upd0[p + 2], None)
            left[p] = rest
            upd1[p] = factors[0][0] * centre + factors[0][1] * rest

        @pl.loop(1, SX + 3, unroll=5)
        def _(p):
            centre = upd1[p]
            rest = (left[p] - centre) + scaled(p, upd1[p - 1], centre, upd1[p + 1], None)
            left[p] = rest
            upd2[p] = factors[1][0] * centre + factors[1][1] * rest

        @pl.loop(2, SX + 2, unroll=4)
        def _(p):
            centre = upd2[p]
            rest = (left[p] - centre) + scaled(p, upd2[p - 1], centre, upd2[p + 1], None)
            upd3 = factors[2][0] * centre + factors[2][1] * rest
            value = ((upd0[p + 1] + upd1[p]) + (centre + upd3)) + ext[p + 1]
            out_ref[p - 1] = value
            inner = value[4:20]
            own_ref[p - 2] = inner
            face_plo[turn, p - 2] = inner[0:1]
            face_phi[turn, p - 2] = inner[15:16]

    def face_place(slot, dst):
        zero4 = jnp.zeros((4, NZ), F32)
        dst[0] = jnp.where(has_w, jnp.concatenate([zero4, face[slot, 0], zero4], axis=0), 0.0)
        dst[SX + 1] = jnp.where(has_e, jnp.concatenate([zero4, face[slot, 1], zero4], axis=0), 0.0)
        rows = iota((ROWS, NZ), 0)

        @pl.loop(0, SX, unroll=2)
        def _(x):
            low = jnp.broadcast_to(jnp.where(has_s, face_lo[slot, x], 0.0), (ROWS, NZ))
            high = jnp.broadcast_to(jnp.where(has_n, face_hi[slot, x], 0.0), (ROWS, NZ))
            value = dst[x + 1]
            dst[x + 1] = jnp.where(rows == 3, low, jnp.where(rows == 20, high, value))

    def q_assemble(low, mid, high):
        @pl.loop(0, SX + 4)
        def _(p):
            q24[p] = padded(low(p), mid(p), high(p))

    upd0[0] = jnp.zeros((ROWS, NZ), F32)
    upd0[SX + 5] = jnp.zeros((ROWS, NZ), F32)
    table = lax.div(iota((KD * 16, 128), 0), 16) == lax.rem(iota((KD * 16, 128), 1), KD)
    pick[...] = jnp.where(table, 1.0, 0.0).astype(BF16)
    loads[0].wait()
    row = restrict(lambda x: base[3, DEPTH + x], FIRST_EXACT, (loads[1], loads[2]))
    greetings = (ZG - 1) + (group - 1) + len(AROUND)
    pl.semaphore_wait(barrier, greetings)
    line_send(0, row)
    loads[3].wait()

    @pl.loop(0, SX)
    def _(x):
        for c in range(4):
            plane = base[c, DEPTH + x]
            base_plo[c, x] = plane[0:2]
            base_phi[c, x] = plane[14:16]

    every = (slice(None),)
    base_halo = (0, DEPTH, base, base_lo, base_hi, base_plo, base_phi, every)
    img_halo = (3, DEPTH, img, img_lo, img_hi, img_plo, img_phi)

    def corr_halo(turn):
        return (1 + turn, 3, corr.at[turn], corr_lo.at[turn], corr_hi.at[turn],
                corr_plo.at[turn], corr_phi.at[turn])

    halo("start", *base_halo)
    line_wait(0)
    group_send(0, quads(0))
    halo("recv", *base_halo)

    rows = iota((ROWS, NZ), 0)
    cols = iota((ROWS, NZ), 1)
    keep_y = ((rows >= 4) & (rows < 20)) | ((rows >= 2) & (rows < 4) & has_s)
    keep_y = keep_y | ((rows >= 20) & (rows < 22) & has_n)

    @pl.loop(0, SX + 4)
    def _(p):
        keep = keep_y & ((p >= DEPTH) | has_w) & ((p < SX + DEPTH) | has_e)
        w0, w1, w2, r = [
            jnp.where(keep, padded(base_lo[c, p], base[c, p], base_hi[c, p]), 0.0)
            for c in range(4)
        ]
        diagonal = 6.0 + w0 + w1 + w2
        jdiag = jnp.where(keep, 1.0 / diagonal, 0.0)
        c0, c1 = 1.0 + w0, 1.0 + w1
        c2 = jnp.where(cols == 0, 0.0, 1.0 + w2)
        scale[0, p] = jdiag
        scale[1, p] = jdiag * c0
        scale[2, p] = jdiag * c1
        scale[3, p] = jdiag * c2
        q24[p] = r

        @pl.when((p >= DEPTH) & (p < SX + DEPTH))
        def _():
            coef[0, p - DEPTH] = diagonal
            coef[1, p - DEPTH] = c0
            coef[2, p - DEPTH] = c1
            coef[3, p - DEPTH] = c2

    loads[4].wait()

    def precondition(turn, out_ref, own_ref, exact):
        group_wait(turn)
        lhs = solve(turn, exact)
        for x in range(SX):
            out = jnp.dot(lhs[:, :256], weights(0, x), preferred_element_type=F32)
            out = out + jnp.dot(lhs[:, 256:], weights(1, x), preferred_element_type=F32)
            if exact:
                out = out[:16] + out[16:]
            corr[turn, 3 + x] = out
            corr_plo[turn, x] = out[0:4]
            corr_phi[turn, x] = out[12:16]
        halo("start", *corr_halo(turn))
        halo("recv", *corr_halo(turn))
        smooth(turn, out_ref, own_ref)
        face_own[turn, 0] = own_ref[0]
        face_own[turn, 1] = own_ref[SX - 1]
        faces("start", turn)
        faces("recv", turn)
        face_place(turn, out_ref)

    precondition(0, search, s_ref, FIRST_EXACT)

    @pl.loop(0, SX, unroll=2)
    def _(x):
        inner = operator(x, search)[4:20]
        img[DEPTH + x] = inner
        i_ref[x] = inner
        img_plo[x] = inner[0:2]
        img_phi[x] = inner[14:16]

    row = restrict(lambda x: img[DEPTH + x], True)
    line_send(1, row)
    halo("start", *img_halo)
    line_wait(1)
    group_send(1, quads(1))
    halo("recv", *img_halo)
    keep_q = keep_y

    @pl.loop(0, SX + 4)
    def _(p):
        keep = keep_q & ((p >= DEPTH) | has_w) & ((p < SX + DEPTH) | has_e)
        q24[p] = jnp.where(keep, padded(img_lo[p], img[p], img_hi[p]), 0.0)

    precondition(1, wfield, w_ref, True)

    zero = jnp.zeros((8, NZ), F32)

    def fold(value):
        return value[0:8] + value[8:16]

    def products(x, sums):
        v = operator(x, wfield)[4:20]
        v_ref[x] = v
        i = img[DEPTH + x]
        r = base[3, DEPTH + x]
        pairs = [(r, r), (r, i), (i, i), (v, r), (v, i), (v, v)]
        return tuple(s + fold(a * b) for s, (a, b) in zip(sums, pairs))

    sums = lax.fori_loop(0, SX, products, (zero,) * 6, unroll=2)
    lanes = iota((1, 128), 1)
    row = jnp.zeros((1, 128), F32)
    for k, s in enumerate(sums):
        s = jnp.sum(s, axis=0, keepdims=True)
        s = jnp.sum(s, axis=1, keepdims=True)
        row = jnp.where(lanes == k, s, row)
    line_send(2, row)
    line_wait(2)
    total = row_a[2, 0]
    for k in range(1, ZG):
        total = total + row_a[2, k]
    per = ZG // QUAD
    group_send(2, jnp.concatenate([total] * per, axis=0) if per > 1 else total)
    group_wait(2)
    total = jnp.sum(row_b[2], axis=0)[0:1]
    rr, ri, ii, vr, vi, vv = [
        jnp.sum(jnp.where(lanes == k, total, 0.0), axis=1, keepdims=True) for k in range(6)
    ]
    alpha = rr / ri
    cross = (ri - alpha * ii) - alpha * (vr - alpha * vi)
    square = ii - alpha * (2.0 * vi - alpha * vv)
    omega = cross / square
    alpha_ref[...] = alpha
    omega_ref[...] = omega

    for turn in range(3):
        gather_finish(turn)
    halo("send", *base_halo)
    for turn in range(2):
        halo("send", *corr_halo(turn))
        faces("send", turn)
    halo("send", *img_halo)


FIRST_EXACT = False


def solution(mesh):
    ngx, ngy = mesh.shape["gx"], mesh.shape["gy"]
    group = ngx * (ngy // ZG)
    vm = pltpu.VMEM

    def local(right_side, velocity, deflation, inverse_rows):
        out = jax.ShapeDtypeStruct((SX, SY, NZ), F32)
        plane = (ROWS, NZ)
        scratch = [
            vm((KD, SX, SY, NZ), BF16),
            vm(inverse_rows.shape, F32),
            vm((4, SX + 4, SY, NZ), F32),
            vm((4, SX + 4, 2, NZ), F32),
            vm((4, SX + 4, 2, NZ), F32),
            vm((4, SX, 2, NZ), F32),
            vm((4, SX, 2, NZ), F32),
            vm((4, SX) + plane, F32),
            vm((4, SX + 4) + plane, F32),
            vm((KD * 16, 128), BF16),
            vm((SX + 4,) + plane, F32),
            vm((2, SX + 6, SY, NZ), F32),
            vm((2, SX + 6, 4, NZ), F32),
            vm((2, SX + 6, 4, NZ), F32),
            vm((2, SX, 4, NZ), F32),
            vm((2, SX, 4, NZ), F32),
            vm((SX + 6,) + plane, F32),
            vm((SX + 4,) + plane, F32),
            vm((SX + 6,) + plane, F32),
            vm((SX + 4,) + plane, F32),
            vm((SX + 4,) + plane, F32),
            vm((2, 2, SY, NZ), F32),
            vm((2, SX, 1, NZ), F32),
            vm((2, SX, 1, NZ), F32),
            vm((2, 2, SY, NZ), F32),
            vm((2, SX, 1, NZ), F32),
            vm((2, SX, 1, NZ), F32),
            vm((SX + 4, SY, NZ), F32),
            vm((SX + 4, 2, NZ), F32),
            vm((SX + 4, 2, NZ), F32),
            vm((SX, 2, NZ), F32),
            vm((SX, 2, NZ), F32),
            vm((SX + 2,) + plane, F32),
            vm((SX + 2,) + plane, F32),
            vm((3, ZG, 1, 128), F32),
            vm((3, group, ZG // QUAD, 128), F32),
            pltpu.SemaphoreType.DMA((5,)),
            pltpu.SemaphoreType.DMA((3, 2)),
            pltpu.SemaphoreType.DMA((3, 2)),
            pltpu.SemaphoreType.DMA((6, 8)),
            pltpu.SemaphoreType.DMA((6, 8)),
        ]

        def body(*refs):
            kernel(ngx, ngy, *refs)

        s, i, w, v, alpha, omega = pl.pallas_call(
            body,
            name="bicgstab",
            out_shape=(out,) * 4 + (jax.ShapeDtypeStruct((1, 1), F32),) * 2,
            in_specs=[pl.BlockSpec(memory_space=pl.ANY)] * 4,
            out_specs=(pl.BlockSpec(memory_space=vm),) * 6,
            scratch_shapes=scratch,
            compiler_params=pltpu.CompilerParams(collective_id=0, has_side_effects=True),
        )(right_side, velocity, deflation, inverse_rows)
        alpha, omega = alpha[0, 0], omega[0, 0]
        field = alpha * s + omega * (s - alpha * w)
        return field, (right_side - alpha * i) - omega * (i - alpha * v)

    return jax.shard_map(
        local,
        mesh=mesh,
        in_specs=(
            P("gx", "gy", None),
            P(None, "gx", "gy", None),
            P(None, "gx", "gy", None),
            P(("gx", "gy"), None),
        ),
        out_specs=(P("gx", "gy", None), P("gx", "gy", None)),
        check_vma=False,
    )
```

time: 72.4 us -> 65 us (0.90)
  Pallas kernels: 68.5 us -> 61.2 us
  local copies, waits for them, and re-layouts: 3.14 us -> 0.01 us
  other arithmetic: 0 us -> 3.02 us
    pallas_call x1, Pallas kernels: 68.5 us -> 61.2 us  [local(): pl.pallas_call(body, name='bicgstab', out_shape=(out,) * 4 + (jax.ShapeDt...]
    unnamed x2, local copies, waits for them, and re-layouts: 3.14 us -> 0.01 us
    sub x0 -> x1, other arithmetic: none -> 3.02 us  [local(): return (field, right_side - alpha * i - omega * (i - alpha * v))]
where the time goes in v2:
time: 65 us; the launch traced here: 64.9 us
  Pallas kernels  61.2 us (94%)
  other arithmetic  3.02 us (5%)
  between operations  0.65 us (1%)
    pallas_call x1, Pallas kernels, local(): pl.pallas_call(body, name='bicgstab', out_shape=(out,) * 4 + (jax.ShapeDt...  61.2 us
    sub x1, other arithmetic, local(): return (field, right_side - alpha * i - omega * (i - alpha * v))  3.02 us

profile of v2, /device:TPU:1, one launch (start us, length us, event | category | flops | bytes accessed | tf_op | source)
XLA Modules:
  0.0 64.9 jit_solution(1436443825473501961)
XLA Ops:
  0.6 0.0 copy-start
  0.6 61.2 %bicgstab.1 = (f32[8,16,256]{2,1,0:T(8,128)}, f32[8,16,256]{2,1,0:T(8,128)}, f32[8,16,256]{2,1,0:T(8,128)}, f32[8,16,256]{2,1,0:T(8,128)}, f32[1,1]{1,0:T(1,128)}, /*index=5*/f32[1,1]{1,0:T(1,128)}) custom-call(f32[8,16,256]{2,1,0:T(8,128)} %refs_0_.1, f32[3,8,16,256]{3,2,1,0:T(8,128)} %refs_1_.1, bf16[32,8,16,256]{3,2,1,0:T(8,128)(2,1)} %refs_2_.1, ...), custom_call_target="tpu_custom_call" | custom-call | tf_op jit(solution)/shard_map/bicgstab/pallas_call | solution.py:536
  61.9 0.0 copy-done
  61.9 3.0 %multiply_subtract_fusion = (f32[8,16,256]{2,1,0:T(8,128)}, f32[8,16,256]{2,1,0:T(8,128)}) fusion(f32[8,16,256]{2,1,0:T(8,128)} %get-tuple-element.12, f32[8,16,256]{2,1,0:T(8,128)} %get-tuple-element.13, f32[8,16,256]{2,1,0:T(8,128)S(1)} %copy-done, f32[]{:T(128)} %bitcast.1, f32[]{:T(128)} %bitcast, f32[8,16,256]{2,1,0:T(8,128)} %get-tuple-element.9, ...), kind=kLoop, calls=%fused_computation | loop fusion | flops 360448 | bytes 917512 | tf_op jit(solution)/shard_map/sub | solution.py:547
Async XLA Ops:
  0.6 61.2 %copy-start = (f32[8,16,256]{2,1,0:T(8,128)S(1)}, f32[8,16,256]{2,1,0:T(8,128)}, u32[]{:S(2)}) copy-start(f32[8,16,256]{2,1,0:T(8,128)} %refs_0_.1) | copy-start | bytes 393220

commit v3 on v2

--- a/solution.py
+++ b/solution.py
@@ -16,6 +16,7 @@
 QUAD = 128 // KD
 ROWS = 24
 SIGMA = 1.0 / 0.9
+FAR_FIRST = [4, 3, 5, 2, 6, 1, 7, 0]
 AROUND = [(1, 1), (-1, 1), (1, -1), (-1, -1), (0, 1), (0, -1), (1, 0), (-1, 0)]
 
 
@@ -34,12 +35,12 @@
 
 def kernel(
     ngx, ngy,
-    r_hbm, vel_hbm, defl_hbm, inv_hbm, s_ref, i_ref, w_ref, v_ref, alpha_ref, omega_ref,
+    r_hbm, vel_hbm, defl_hbm, inv_hbm, s_hbm, i_hbm, w_hbm, v_hbm, alpha_ref, omega_ref,
     defl, inv, base, base_lo, base_hi, base_plo, base_phi,
     coef, scale, pick, q24, corr, corr_lo, corr_hi, corr_plo, corr_phi, ext, left, upd0, upd1, upd2,
     face, face_lo, face_hi, face_own, face_plo, face_phi,
-    img, img_lo, img_hi, img_plo, img_phi, search, wfield, row_a, row_b,
-    local_sem, ag_send, ag_recv, halo_send, halo_recv,
+    img, img_lo, img_hi, img_plo, img_phi, search, wfield, s_own, w_own, v_own, row_a, row_b, row_all,
+    local_sem, out_sem, ag_send, ag_recv, all_sends, all_recvs, halo_send, halo_recv,
 ):
     gx = lax.axis_index("gx")
     gy = lax.axis_index("gy")
@@ -49,6 +50,7 @@
     line = xpos * ZG
     group = ngx * xg
     seat = gx * xg + xpos
+    number = gx * ngy + gy
     here = (gx, gy)
     barrier = pltpu.get_barrier_semaphore()
 
@@ -93,35 +95,58 @@
             device_id=device, device_id_type=MESH,
         )
 
-    def line_send(turn, row):
-        row_a[turn, zpos] = row
+    def line_send(row):
+        row_a[zpos] = row
 
         @pl.loop(1, ZG)
         def _(step):
-            remote(row_a.at[turn, zpos], row_a.at[turn, zpos], ag_send.at[turn, 0],
-                   ag_recv.at[turn, 0], line_peer(step)).start()
-
-    def line_wait(turn):
-        view = row_a.at[turn, pl.ds(0, ZG - 1)]
-        remote(view, view, ag_send.at[turn, 0], ag_recv.at[turn, 0], here).wait_recv()
-
-    def group_send(turn, rows):
-        row_b[turn, seat] = rows
+            remote(row_a.at[zpos], row_a.at[zpos], ag_send.at[0], ag_recv.at[0],
+                   line_peer(step)).start()
+
+    def line_wait():
+        view = row_a.at[pl.ds(0, ZG - 1)]
+        remote(view, view, ag_send.at[0], ag_recv.at[0], here).wait_recv()
+
+    def group_send(rows):
+        row_b[seat] = rows
 
         @pl.loop(1, group)
         def _(step):
-            remote(row_b.at[turn, seat], row_b.at[turn, seat], ag_send.at[turn, 1],
-                   ag_recv.at[turn, 1], group_peer(step)).start()
-
-    def group_wait(turn):
-        view = row_b.at[turn, pl.ds(0, group - 1)]
-        remote(view, view, ag_send.at[turn, 1], ag_recv.at[turn, 1], here).wait_recv()
-
-    def gather_finish(turn):
-        view = row_a.at[turn, pl.ds(0, ZG - 1)]
-        remote(view, view, ag_send.at[turn, 0], ag_recv.at[turn, 0], here).wait_send()
-        view = row_b.at[turn, pl.ds(0, group - 1)]
-        remote(view, view, ag_send.at[turn, 1], ag_recv.at[turn, 1], here).wait_send()
+            remote(row_b.at[seat], row_b.at[seat], ag_send.at[1], ag_recv.at[1],
+                   group_peer(step)).start()
+
+    def group_wait():
+        view = row_b.at[pl.ds(0, group - 1)]
+        remote(view, view, ag_send.at[1], ag_recv.at[1], here).wait_recv()
+
+    def all_send(turn, row):
+        slot = turn - 1
+        row_all[slot, number] = row
+
+        for dz in FAR_FIRST:
+            side = lax.rem(zpos + dz, ZG)
+
+            @pl.loop(0 if dz else 1, group, unroll=8 if dz else 1)
+            def _(step):
+                other = lax.rem(seat + step, group)
+                device = (lax.div(other, xg), lax.rem(other, xg) * ZG + side)
+                remote(row_all.at[slot, number], row_all.at[slot, number], all_sends.at[slot],
+                       all_recvs.at[slot], device).start()
+
+    def all_wait(turn, what="recv"):
+        slot = turn - 1
+        view = row_all.at[slot, pl.ds(0, ngx * ngy - 1)]
+        copy = remote(view, view, all_sends.at[slot], all_recvs.at[slot], here)
+        if what == "recv":
+            copy.wait_recv()
+        else:
+            copy.wait_send()
+
+    def first_finish():
+        view = row_a.at[pl.ds(0, ZG - 1)]
+        remote(view, view, ag_send.at[0], ag_recv.at[0], here).wait_send()
+        view = row_b.at[pl.ds(0, group - 1)]
+        remote(view, view, ag_send.at[1], ag_recv.at[1], here).wait_send()
 
     def beside(dx, dy):
         tests = {(-1, 0): has_w, (1, 0): has_e, (0, -1): has_s, (0, 1): has_n}
@@ -223,12 +248,12 @@
         mine = lax.div(iota((1, 128), 1), KD) == lax.rem(zpos, QUAD)
         return jnp.where(mine, row, 0.0)
 
-    def quads(turn):
+    def quads():
         rows = []
         for start in range(0, ZG, QUAD):
-            total = row_a[turn, start]
+            total = row_a[start]
             for k in range(1, QUAD):
-                total = total + row_a[turn, start + k]
+                total = total + row_a[start + k]
             rows.append(total)
         return jnp.concatenate(rows, axis=0) if len(rows) > 1 else rows[0]
 
@@ -236,7 +261,11 @@
         per = ZG // QUAD
         sums = [jnp.zeros((KD, 128), F32) for _ in range(4)]
         for j in range(group * per):
-            value = row_b[turn, j // per, pl.ds(j % per, 1), :]
+            if turn == 0:
+                value = row_b[j // per, pl.ds(j % per, 1), :]
+            else:
+                first, second, third, fourth = [row_all[0, QUAD * j + k] for k in range(QUAD)]
+                value = (first + second) + (third + fourth)
             sums[j % 4] = sums[j % 4] + inv[:, pl.ds(j * 128, 128)] * value
         total = (sums[0] + sums[1]) + (sums[2] + sums[3])
         solved = jnp.sum(total, axis=1, keepdims=True)
@@ -328,7 +357,7 @@
     row = restrict(lambda x: base[3, DEPTH + x], FIRST_EXACT, (loads[1], loads[2]))
     greetings = (ZG - 1) + (group - 1) + len(AROUND)
     pl.semaphore_wait(barrier, greetings)
-    line_send(0, row)
+    line_send(row)
     loads[3].wait()
 
     @pl.loop(0, SX)
@@ -347,8 +376,8 @@
                 corr_plo.at[turn], corr_phi.at[turn])
 
     halo("start", *base_halo)
-    line_wait(0)
-    group_send(0, quads(0))
+    line_wait()
+    group_send(quads())
     halo("recv", *base_halo)
 
     rows = iota((ROWS, NZ), 0)
@@ -382,8 +411,10 @@
 
     loads[4].wait()
 
+    def emit(k, src, dst):
+        pltpu.make_async_copy(src, dst, out_sem.at[k]).start()
+
     def precondition(turn, out_ref, own_ref, exact):
-        group_wait(turn)
         lhs = solve(turn, exact)
         for x in range(SX):
             out = jnp.dot(lhs[:, :256], weights(0, x), preferred_element_type=F32)
@@ -402,21 +433,21 @@
         faces("recv", turn)
         face_place(turn, out_ref)
 
-    precondition(0, search, s_ref, FIRST_EXACT)
+    group_wait()
+    precondition(0, search, s_own, FIRST_EXACT)
+    emit(0, s_own, s_hbm)
 
     @pl.loop(0, SX, unroll=2)
     def _(x):
         inner = operator(x, search)[4:20]
         img[DEPTH + x] = inner
-        i_ref[x] = inner
         img_plo[x] = inner[0:2]
         img_phi[x] = inner[14:16]
 
     row = restrict(lambda x: img[DEPTH + x], True)
-    line_send(1, row)
+    all_send(1, row)
     halo("start", *img_halo)
-    line_wait(1)
-    group_send(1, quads(1))
+    emit(1, img.at[own], i_hbm)
     halo("recv", *img_halo)
     keep_q = keep_y
 
@@ -425,7 +456,8 @@
         keep = keep_q & ((p >= DEPTH) | has_w) & ((p < SX + DEPTH) | has_e)
         q24[p] = jnp.where(keep, padded(img_lo[p], img[p], img_hi[p]), 0.0)
 
-    precondition(1, wfield, w_ref, True)
+    all_wait(1)
+    precondition(1, wfield, w_own, True)
 
     zero = jnp.zeros((8, NZ), F32)
 
@@ -434,7 +466,7 @@
 
     def products(x, sums):
         v = operator(x, wfield)[4:20]
-        v_ref[x] = v
+        v_own[x] = v
         i = img[DEPTH + x]
         r = base[3, DEPTH + x]
         pairs = [(r, r), (r, i), (i, i), (v, r), (v, i), (v, v)]
@@ -447,15 +479,16 @@
         s = jnp.sum(s, axis=0, keepdims=True)
         s = jnp.sum(s, axis=1, keepdims=True)
         row = jnp.where(lanes == k, s, row)
-    line_send(2, row)
-    line_wait(2)
-    total = row_a[2, 0]
-    for k in range(1, ZG):
-        total = total + row_a[2, k]
-    per = ZG // QUAD
-    group_send(2, jnp.concatenate([total] * per, axis=0) if per > 1 else total)
-    group_wait(2)
-    total = jnp.sum(row_b[2], axis=0)[0:1]
+    all_send(2, row)
+    emit(2, w_own, w_hbm)
+    emit(3, v_own, v_hbm)
+    all_wait(2)
+    parts = [jnp.zeros((1, 128), F32) for _ in range(8)]
+    for j in range(ngx * ngy):
+        parts[j % 8] = parts[j % 8] + row_all[1, j]
+    while len(parts) > 1:
+        parts = [parts[k] + parts[k + 1] for k in range(0, len(parts), 2)]
+    total = parts[0]
     rr, ri, ii, vr, vi, vv = [
         jnp.sum(jnp.where(lanes == k, total, 0.0), axis=1, keepdims=True) for k in range(6)
     ]
@@ -466,8 +499,13 @@
     alpha_ref[...] = alpha
     omega_ref[...] = omega
 
-    for turn in range(3):
-        gather_finish(turn)
+    for k, (src, dst) in enumerate(
+        [(s_own, s_hbm), (img.at[own], i_hbm), (w_own, w_hbm), (v_own, v_hbm)]
+    ):
+        pltpu.make_async_copy(src, dst, out_sem.at[k]).wait()
+    first_finish()
+    all_wait(1, "send")
+    all_wait(2, "send")
     halo("send", *base_halo)
     for turn in range(2):
         halo("send", *corr_halo(turn))
@@ -521,11 +559,18 @@
             vm((SX, 2, NZ), F32),
             vm((SX + 2,) + plane, F32),
             vm((SX + 2,) + plane, F32),
-            vm((3, ZG, 1, 128), F32),
-            vm((3, group, ZG // QUAD, 128), F32),
+            vm((SX, SY, NZ), F32),
+            vm((SX, SY, NZ), F32),
+            vm((SX, SY, NZ), F32),
+            vm((ZG, 1, 128), F32),
+            vm((group, ZG // QUAD, 128), F32),
+            vm((2, ngx * ngy, 1, 128), F32),
             pltpu.SemaphoreType.DMA((5,)),
-            pltpu.SemaphoreType.DMA((3, 2)),
-            pltpu.SemaphoreType.DMA((3, 2)),
+            pltpu.SemaphoreType.DMA((4,)),
+            pltpu.SemaphoreType.DMA((2,)),
+            pltpu.SemaphoreType.DMA((2,)),
+            pltpu.SemaphoreType.DMA((2,)),
+            pltpu.SemaphoreType.DMA((2,)),
             pltpu.SemaphoreType.DMA((6, 8)),
             pltpu.SemaphoreType.DMA((6, 8)),
         ]
@@ -538,7 +583,7 @@
             name="bicgstab",
             out_shape=(out,) * 4 + (jax.ShapeDtypeStruct((1, 1), F32),) * 2,
             in_specs=[pl.BlockSpec(memory_space=pl.ANY)] * 4,
-            out_specs=(pl.BlockSpec(memory_space=vm),) * 6,
+            out_specs=(pl.BlockSpec(memory_space=pl.ANY),) * 4 + (pl.BlockSpec(memory_space=vm),) * 2,
             scratch_shapes=scratch,
             compiler_params=pltpu.CompilerParams(collective_id=0, has_side_effects=True),
         )(right_side, velocity, deflation, inverse_rows)

time: 65 us -> 62.5 us (0.962)
  Pallas kernels: 61.2 us -> 58.7 us
    pallas_call x1, Pallas kernels: 61.2 us -> 58.7 us  [local(): pl.pallas_call(body, name='bicgstab', out_shape=(out,) * 4 + (jax.ShapeDt...]
where the time goes in v3:
time: 62.5 us; the launch traced here: 62.4 us
  Pallas kernels  58.7 us (94%)
  other arithmetic  3.02 us (5%)
  between operations  0.65 us (1%)
    pallas_call x1, Pallas kernels, local(): pl.pallas_call(body, name='bicgstab', out_shape=(out,) * 4 + (jax.ShapeDt...  58.7 us
    sub x1, other arithmetic, local(): return (field, right_side - alpha * i - omega * (i - alpha * v))  3.02 us

profile of v3, /device:TPU:1, one launch (start us, length us, event | category | flops | bytes accessed | tf_op | source)
XLA Modules:
  0.0 62.4 jit_solution(18371287092341085057)
XLA Ops:
  0.6 0.0 copy-start
  0.6 58.7 %bicgstab.1 = (f32[8,16,256]{2,1,0:T(8,128)}, f32[8,16,256]{2,1,0:T(8,128)}, f32[8,16,256]{2,1,0:T(8,128)}, f32[8,16,256]{2,1,0:T(8,128)}, f32[1,1]{1,0:T(1,128)}, /*index=5*/f32[1,1]{1,0:T(1,128)}) custom-call(f32[8,16,256]{2,1,0:T(8,128)} %refs_0_.1, f32[3,8,16,256]{3,2,1,0:T(8,128)} %refs_1_.1, bf16[32,8,16,256]{3,2,1,0:T(8,128)(2,1)} %refs_2_.1, ...), custom_call_target="tpu_custom_call" | custom-call | tf_op jit(solution)/shard_map/bicgstab/pallas_call | solution.py:581
  59.4 0.0 copy-done
  59.4 3.0 %multiply_subtract_fusion = (f32[8,16,256]{2,1,0:T(8,128)}, f32[8,16,256]{2,1,0:T(8,128)}) fusion(f32[8,16,256]{2,1,0:T(8,128)} %get-tuple-element.12, f32[8,16,256]{2,1,0:T(8,128)} %get-tuple-element.13, f32[8,16,256]{2,1,0:T(8,128)S(1)} %copy-done, f32[]{:T(128)} %bitcast.1, f32[]{:T(128)} %bitcast, f32[8,16,256]{2,1,0:T(8,128)} %get-tuple-element.9, ...), kind=kLoop, calls=%fused_computation | loop fusion | flops 360448 | bytes 917512 | tf_op jit(solution)/shard_map/sub | solution.py:592
Async XLA Ops:
  0.6 58.7 %copy-start = (f32[8,16,256]{2,1,0:T(8,128)S(1)}, f32[8,16,256]{2,1,0:T(8,128)}, u32[]{:S(2)}) copy-start(f32[8,16,256]{2,1,0:T(8,128)} %refs_0_.1) | copy-start | bytes 393220

commit v4 on v3

--- a/solution.py
+++ b/solution.py
@@ -35,12 +35,12 @@
 
 def kernel(
     ngx, ngy,
-    r_hbm, vel_hbm, defl_hbm, inv_hbm, s_hbm, i_hbm, w_hbm, v_hbm, alpha_ref, omega_ref,
+    r_hbm, vel_hbm, defl_hbm, inv_hbm, both,
     defl, inv, base, base_lo, base_hi, base_plo, base_phi,
     coef, scale, pick, q24, corr, corr_lo, corr_hi, corr_plo, corr_phi, ext, left, upd0, upd1, upd2,
     face, face_lo, face_hi, face_own, face_plo, face_phi,
     img, img_lo, img_hi, img_plo, img_phi, search, wfield, s_own, w_own, v_own, row_a, row_b, row_all,
-    local_sem, out_sem, ag_send, ag_recv, all_sends, all_recvs, halo_send, halo_recv,
+    local_sem, ag_send, ag_recv, all_sends, all_recvs, halo_send, halo_recv,
 ):
     gx = lax.axis_index("gx")
     gy = lax.axis_index("gy")
@@ -411,9 +411,6 @@
 
     loads[4].wait()
 
-    def emit(k, src, dst):
-        pltpu.make_async_copy(src, dst, out_sem.at[k]).start()
-
     def precondition(turn, out_ref, own_ref, exact):
         lhs = solve(turn, exact)
         for x in range(SX):
@@ -435,7 +432,6 @@
 
     group_wait()
     precondition(0, search, s_own, FIRST_EXACT)
-    emit(0, s_own, s_hbm)
 
     @pl.loop(0, SX, unroll=2)
     def _(x):
@@ -447,7 +443,6 @@
     row = restrict(lambda x: img[DEPTH + x], True)
     all_send(1, row)
     halo("start", *img_halo)
-    emit(1, img.at[own], i_hbm)
     halo("recv", *img_halo)
     keep_q = keep_y
 
@@ -480,8 +475,6 @@
         s = jnp.sum(s, axis=1, keepdims=True)
         row = jnp.where(lanes == k, s, row)
     all_send(2, row)
-    emit(2, w_own, w_hbm)
-    emit(3, v_own, v_hbm)
     all_wait(2)
     parts = [jnp.zeros((1, 128), F32) for _ in range(8)]
     for j in range(ngx * ngy):
@@ -496,13 +489,11 @@
     cross = (ri - alpha * ii) - alpha * (vr - alpha * vi)
     square = ii - alpha * (2.0 * vi - alpha * vv)
     omega = cross / square
-    alpha_ref[...] = alpha
-    omega_ref[...] = omega
-
-    for k, (src, dst) in enumerate(
-        [(s_own, s_hbm), (img.at[own], i_hbm), (w_own, w_hbm), (v_own, v_hbm)]
-    ):
-        pltpu.make_async_copy(src, dst, out_sem.at[k]).wait()
+    for x in range(SX):
+        sv, iv = s_own[x], img[DEPTH + x]
+        both[0, x] = alpha * sv + omega * (sv - alpha * w_own[x])
+        both[1, x] = (base[3, DEPTH + x] - alpha * iv) - omega * (iv - alpha * v_own[x])
+
     first_finish()
     all_wait(1, "send")
     all_wait(2, "send")
@@ -566,7 +557,6 @@
             vm((group, ZG // QUAD, 128), F32),
             vm((2, ngx * ngy, 1, 128), F32),
             pltpu.SemaphoreType.DMA((5,)),
-            pltpu.SemaphoreType.DMA((4,)),
             pltpu.SemaphoreType.DMA((2,)),
             pltpu.SemaphoreType.DMA((2,)),
             pltpu.SemaphoreType.DMA((2,)),
@@ -578,18 +568,16 @@
         def body(*refs):
             kernel(ngx, ngy, *refs)
 
-        s, i, w, v, alpha, omega = pl.pallas_call(
+        both = pl.pallas_call(
             body,
             name="bicgstab",
-            out_shape=(out,) * 4 + (jax.ShapeDtypeStruct((1, 1), F32),) * 2,
+            out_shape=jax.ShapeDtypeStruct((2, SX, SY, NZ), F32),
             in_specs=[pl.BlockSpec(memory_space=pl.ANY)] * 4,
-            out_specs=(pl.BlockSpec(memory_space=pl.ANY),) * 4 + (pl.BlockSpec(memory_space=vm),) * 2,
+            out_specs=pl.BlockSpec(memory_space=vm),
             scratch_shapes=scratch,
             compiler_params=pltpu.CompilerParams(collective_id=0, has_side_effects=True),
         )(right_side, velocity, deflation, inverse_rows)
-        alpha, omega = alpha[0, 0], omega[0, 0]
-        field = alpha * s + omega * (s - alpha * w)
-        return field, (right_side - alpha * i) - omega * (i - alpha * v)
+        return both[0], both[1]
 
     return jax.shard_map(
         local,

time: 62.5 us -> 61.3 us (0.981)
  other arithmetic: 3.02 us -> 0 us
  local copies, waits for them, and re-layouts: 0.01 us -> 1.69 us
    sub x1 -> x0, other arithmetic: 3.02 us -> none  [local(): return (field, right_side - alpha * i - omega * (i - alpha * v))]
    squeeze x0 -> x1, local copies, waits for them, and re-layouts: none -> 1.69 us  [local(): return (both[0], both[1])]
where the time goes in v4:
time: 61.3 us; the launch traced here: 61.2 us
  Pallas kernels  58.8 us (96%)
  local copies, waits for them, and re-layouts  1.69 us (3%)
  between operations  0.64 us (1%)
    pallas_call x1, Pallas kernels, local(): pl.pallas_call(body, name='bicgstab', out_shape=jax.ShapeDtypeStruct((2,...  58.8 us
    squeeze x1, local copies, waits for them, and re-layouts, local(): return (both[0], both[1])  1.69 us

profile of v4, /device:TPU:1, one launch (start us, length us, event | category | flops | bytes accessed | tf_op | source)
XLA Modules:
  0.0 61.2 jit_solution(12284036873531869347)
XLA Ops:
  0.6 58.8 %bicgstab.1 = f32[2,8,16,256]{3,2,1,0:T(8,128)} custom-call(f32[8,16,256]{2,1,0:T(8,128)} %refs_0_.1, f32[3,8,16,256]{3,2,1,0:T(8,128)} %refs_1_.1, bf16[32,8,16,256]{3,2,1,0:T(8,128)(2,1)} %refs_2_.1, f32[32,8192]{1,0:T(8,128)} %refs_3_.1), custom_call_target="tpu_custom_call" | custom-call | tf_op jit(solution)/shard_map/bicgstab/pallas_call | solution.py:571
  59.5 1.7 %slice_bitcast_fusion = (f32[8,16,256]{2,1,0:T(8,128)}, f32[8,16,256]{2,1,0:T(8,128)}) fusion(f32[2,8,16,256]{3,2,1,0:T(8,128)} %bicgstab.1), kind=kLoop, calls=%fused_computation | loop fusion | bytes 524288 | tf_op jit(solution)/shard_map/squeeze | solution.py:580

commit v5 on v4

--- a/solution.py
+++ b/solution.py
@@ -36,7 +36,7 @@
 def kernel(
     ngx, ngy,
     r_hbm, vel_hbm, defl_hbm, inv_hbm, both,
-    defl, inv, base, base_lo, base_hi, base_plo, base_phi,
+    natural, defl, defl_eo, lanes_ref, final, inv, base, base_lo, base_hi, base_plo, base_phi,
     coef, scale, pick, q24, corr, corr_lo, corr_hi, corr_plo, corr_phi, ext, left, upd0, upd1, upd2,
     face, face_lo, face_hi, face_own, face_plo, face_phi,
     img, img_lo, img_hi, img_plo, img_phi, search, wfield, s_own, w_own, v_own, row_a, row_b, row_all,
@@ -66,10 +66,10 @@
 
     own = pl.ds(DEPTH, SX)
     loads = [
-        pltpu.make_async_copy(r_hbm, base.at[3, own], local_sem.at[0]),
+        pltpu.make_async_copy(r_hbm, natural.at[3], local_sem.at[0]),
         pltpu.make_async_copy(defl_hbm.at[pl.ds(0, 16)], defl.at[pl.ds(0, 16)], local_sem.at[1]),
         pltpu.make_async_copy(defl_hbm.at[pl.ds(16, 16)], defl.at[pl.ds(16, 16)], local_sem.at[2]),
-        pltpu.make_async_copy(vel_hbm, base.at[pl.ds(0, 3), own], local_sem.at[3]),
+        pltpu.make_async_copy(vel_hbm, natural.at[pl.ds(0, 3)], local_sem.at[3]),
         pltpu.make_async_copy(inv_hbm, inv, local_sem.at[4]),
     ]
     for load in loads:
@@ -198,15 +198,30 @@
             )
             act(what, copy, dx, dy)
 
-    lane_end = iota((ROWS, NZ), 1) == NZ - 1
+    lane_end = iota((ROWS, 128), 1) == 127
 
     def shifts(before, centre, after, add, c0, c1, c2):
-        ahead = jnp.where(lane_end, 0.0, pltpu.roll(centre, NZ - 1, 1))
+        even, odd = centre[:, :128], centre[:, 128:]
+        beyond = jnp.where(lane_end, 0.0, pltpu.roll(even, 127, 1))
+        ahead = jnp.concatenate([odd, beyond], axis=1)
+        behind = jnp.concatenate([pltpu.roll(odd, 1, 1), even], axis=1)
         nexts = (after + pltpu.roll(centre, ROWS - 1, 0)) + ahead
         if add is not None:
             nexts = nexts + add
         previous = c0 * before + c1 * pltpu.roll(centre, 1, 0)
-        return nexts, previous + c2 * pltpu.roll(centre, 1, 1)
+        return nexts, previous + c2 * behind
+
+    def order(value, back):
+        high = value.astype(BF16)
+        rest = value - high.astype(F32)
+        middle = rest.astype(BF16)
+        low = (rest - middle.astype(F32)).astype(BF16)
+        dims = (((1,), (1 if back else 0,)), ((), ()))
+        high, middle, low = [
+            lax.dot_general(part, lanes_ref[...], dims, preferred_element_type=F32)
+            for part in (high, middle, low)
+        ]
+        return high + (middle + low)
 
     def operator(x, field):
         nexts, previous = shifts(
@@ -219,10 +234,10 @@
         rest = (value - top.astype(F32)).astype(BF16)
         return jnp.concatenate([top, rest], axis=0)
 
-    def weights(half, x):
-        return defl[pl.ds(half * 16, 16), x].reshape(256, NZ)
-
-    def restrict(plane, exact, ready=(None, None)):
+    def weights(vectors, half, x):
+        return vectors[pl.ds(half * 16, 16), x].reshape(256, NZ)
+
+    def restrict(vectors, plane, exact, ready=(None, None)):
         lhs = [split(plane(x)) if exact else plane(x).astype(BF16) for x in range(SX)]
         packed = []
         for half in range(2):
@@ -231,7 +246,7 @@
             total = None
             for x in range(SX):
                 part = lax.dot_general(
-                    lhs[x], weights(half, x), (((1,), (1,)), ((), ())), preferred_element_type=F32
+                    lhs[x], weights(vectors, half, x), (((1,), (1,)), ((), ())), preferred_element_type=F32
                 )
                 total = part if total is None else total + part
             same = lax.rem(iota(total.shape, 0), 16) == lax.rem(iota(total.shape, 1), 16)
@@ -353,8 +368,11 @@
     upd0[SX + 5] = jnp.zeros((ROWS, NZ), F32)
     table = lax.div(iota((KD * 16, 128), 0), 16) == lax.rem(iota((KD * 16, 128), 1), KD)
     pick[...] = jnp.where(table, 1.0, 0.0).astype(BF16)
+    source, place = iota((NZ, NZ), 0), iota((NZ, NZ), 1)
+    table = source == 2 * lax.rem(place, 128) + lax.div(place, 128)
+    lanes_ref[...] = jnp.where(table, 1.0, 0.0).astype(BF16)
     loads[0].wait()
-    row = restrict(lambda x: base[3, DEPTH + x], FIRST_EXACT, (loads[1], loads[2]))
+    row = restrict(defl, lambda x: natural[3, x], FIRST_EXACT, (loads[1], loads[2]))
     greetings = (ZG - 1) + (group - 1) + len(AROUND)
     pl.semaphore_wait(barrier, greetings)
     line_send(row)
@@ -362,8 +380,10 @@
 
     @pl.loop(0, SX)
     def _(x):
+        planes = order(natural[:, x].reshape(4 * SY, NZ), False).reshape(4, SY, NZ)
         for c in range(4):
-            plane = base[c, DEPTH + x]
+            plane = planes[c]
+            base[c, DEPTH + x] = plane
             base_plo[c, x] = plane[0:2]
             base_phi[c, x] = plane[14:16]
 
@@ -409,13 +429,19 @@
             coef[2, p - DEPTH] = c1
             coef[3, p - DEPTH] = c2
 
+    @pl.loop(0, SX)
+    def _(x):
+        for half in range(2):
+            moved = jnp.dot(weights(defl, half, x), lanes_ref[...], preferred_element_type=F32)
+            defl_eo[pl.ds(half * 16, 16), x] = moved.astype(BF16).reshape(16, SY, NZ)
+
     loads[4].wait()
 
     def precondition(turn, out_ref, own_ref, exact):
         lhs = solve(turn, exact)
         for x in range(SX):
-            out = jnp.dot(lhs[:, :256], weights(0, x), preferred_element_type=F32)
-            out = out + jnp.dot(lhs[:, 256:], weights(1, x), preferred_element_type=F32)
+            out = jnp.dot(lhs[:, :256], weights(defl_eo, 0, x), preferred_element_type=F32)
+            out = out + jnp.dot(lhs[:, 256:], weights(defl_eo, 1, x), preferred_element_type=F32)
             if exact:
                 out = out[:16] + out[16:]
             corr[turn, 3 + x] = out
@@ -440,7 +466,7 @@
         img_plo[x] = inner[0:2]
         img_phi[x] = inner[14:16]
 
-    row = restrict(lambda x: img[DEPTH + x], True)
+    row = restrict(defl_eo, lambda x: img[DEPTH + x], True)
     all_send(1, row)
     halo("start", *img_halo)
     halo("recv", *img_halo)
@@ -475,6 +501,12 @@
         s = jnp.sum(s, axis=1, keepdims=True)
         row = jnp.where(lanes == k, s, row)
     all_send(2, row)
+
+    @pl.loop(0, SX)
+    def _(x):
+        fields = [s_own[x], img[DEPTH + x], w_own[x], v_own[x]]
+        final[:, x] = order(jnp.concatenate(fields, axis=0), True).reshape(4, SY, NZ)
+
     all_wait(2)
     parts = [jnp.zeros((1, 128), F32) for _ in range(8)]
     for j in range(ngx * ngy):
@@ -490,9 +522,9 @@
     square = ii - alpha * (2.0 * vi - alpha * vv)
     omega = cross / square
     for x in range(SX):
-        sv, iv = s_own[x], img[DEPTH + x]
-        both[0, x] = alpha * sv + omega * (sv - alpha * w_own[x])
-        both[1, x] = (base[3, DEPTH + x] - alpha * iv) - omega * (iv - alpha * v_own[x])
+        sv, iv, wv, vv = final[0, x], final[1, x], final[2, x], final[3, x]
+        both[0, x] = alpha * sv + omega * (sv - alpha * wv)
+        both[1, x] = (natural[3, x] - alpha * iv) - omega * (iv - alpha * vv)
 
     first_finish()
     all_wait(1, "send")
@@ -516,7 +548,11 @@
         out = jax.ShapeDtypeStruct((SX, SY, NZ), F32)
         plane = (ROWS, NZ)
         scratch = [
+            vm((4, SX, SY, NZ), F32),
             vm((KD, SX, SY, NZ), BF16),
+            vm((KD, SX, SY, NZ), BF16),
+            vm((NZ, NZ), BF16),
+            vm((4, SX, SY, NZ), F32),
             vm(inverse_rows.shape, F32),
             vm((4, SX + 4, SY, NZ), F32),
             vm((4, SX + 4, 2, NZ), F32),

time: 61.3 us -> 60.6 us (0.989)
  Pallas kernels: 58.8 us -> 58.1 us
    pallas_call x1, Pallas kernels: 58.8 us -> 58.1 us  [local(): pl.pallas_call(body, name='bicgstab', out_shape=jax.ShapeDtypeStruct((2,...]
where the time goes in v5:
time: 60.6 us; the launch traced here: 60.5 us
  Pallas kernels  58.1 us (96%)
  local copies, waits for them, and re-layouts  1.69 us (3%)
  between operations  0.64 us (1%)
    pallas_call x1, Pallas kernels, local(): pl.pallas_call(body, name='bicgstab', out_shape=jax.ShapeDtypeStruct((2,...  58.1 us
    squeeze x1, local copies, waits for them, and re-layouts, local(): return (both[0], both[1])  1.69 us

profile of v5, /device:TPU:1, one launch (start us, length us, event | category | flops | bytes accessed | tf_op | source)
XLA Modules:
  0.0 60.5 jit_solution(11584014663543278124)
XLA Ops:
  0.6 58.1 %bicgstab.1 = f32[2,8,16,256]{3,2,1,0:T(8,128)} custom-call(f32[8,16,256]{2,1,0:T(8,128)} %refs_0_.1, f32[3,8,16,256]{3,2,1,0:T(8,128)} %refs_1_.1, bf16[32,8,16,256]{3,2,1,0:T(8,128)(2,1)} %refs_2_.1, f32[32,8192]{1,0:T(8,128)} %refs_3_.1), custom_call_target="tpu_custom_call" | custom-call | tf_op jit(solution)/shard_map/bicgstab/pallas_call | solution.py:607
  58.8 1.7 %slice_bitcast_fusion = (f32[8,16,256]{2,1,0:T(8,128)}, f32[8,16,256]{2,1,0:T(8,128)}) fusion(f32[2,8,16,256]{3,2,1,0:T(8,128)} %bicgstab.1), kind=kLoop, calls=%fused_computation | loop fusion | bytes 524288 | tf_op jit(solution)/shard_map/squeeze | solution.py:616

commit v6 on v5

--- a/solution.py
+++ b/solution.py
@@ -16,7 +16,14 @@
 QUAD = 128 // KD
 ROWS = 24
 SIGMA = 1.0 / 0.9
-FAR_FIRST = [4, 3, 5, 2, 6, 1, 7, 0]
+
+
+def hops(step, ring):
+    return min(step, ring - step)
+
+
+def near_last(ring):
+    return sorted(range(ring), key=lambda step: -hops(step, ring))
 AROUND = [(1, 1), (-1, 1), (1, -1), (-1, -1), (0, 1), (0, -1), (1, 0), (-1, 0)]
 
 
@@ -57,9 +64,30 @@
     def line_peer(step):
         return (gx, line + lax.rem(zpos + step, ZG))
 
-    def group_peer(step):
-        other = lax.rem(seat + step, group)
-        return (lax.div(other, xg), lax.rem(other, xg) * ZG + zpos)
+    def spread(act, dz, dx):
+        other = lax.rem(xpos + dx, xg) * ZG + lax.rem(zpos + dz, ZG)
+
+        @pl.loop(0, ngx, unroll=ngx)
+        def _(step):
+            act((lax.rem(gx + step + ngx // 2, ngx), other))
+
+    def group_each(act):
+        for dx in near_last(xg):
+            if dx:
+                spread(act, 0, dx)
+        mine(act)
+
+    def mine(act):
+        @pl.loop(1, ngx, unroll=ngx - 1)
+        def _(step):
+            act((lax.rem(gx + step, ngx), gy))
+
+    def all_each(act):
+        pairs = [(dz, dx) for dz in range(ZG) for dx in range(xg) if dz or dx]
+        pairs.sort(key=lambda p: -hops(p[0], ZG) - hops(p[1], xg))
+        for dz, dx in pairs:
+            spread(act, dz, dx)
+        mine(act)
 
     def greet(device):
         pl.semaphore_signal(barrier, inc=1, device_id=device, device_id_type=MESH)
@@ -75,13 +103,10 @@
     for load in loads:
         load.start()
 
-    @pl.loop(1, ZG)
-    def _(step):
-        greet(line_peer(step))
-
-    @pl.loop(1, group)
-    def _(step):
-        greet(group_peer(step))
+    for step in near_last(ZG):
+        if step:
+            greet(line_peer(step))
+    group_each(greet)
 
     for dx, dy in AROUND:
         greet((lax.rem(gx + dx + ngx, ngx), lax.rem(gy + dy + ngy, ngy)))
@@ -98,10 +123,10 @@
     def line_send(row):
         row_a[zpos] = row
 
-        @pl.loop(1, ZG)
-        def _(step):
-            remote(row_a.at[zpos], row_a.at[zpos], ag_send.at[0], ag_recv.at[0],
-                   line_peer(step)).start()
+        for step in near_last(ZG):
+            if step:
+                remote(row_a.at[zpos], row_a.at[zpos], ag_send.at[0], ag_recv.at[0],
+                       line_peer(step)).start()
 
     def line_wait():
         view = row_a.at[pl.ds(0, ZG - 1)]
@@ -110,10 +135,8 @@
     def group_send(rows):
         row_b[seat] = rows
 
-        @pl.loop(1, group)
-        def _(step):
-            remote(row_b.at[seat], row_b.at[seat], ag_send.at[1], ag_recv.at[1],
-                   group_peer(step)).start()
+        group_each(lambda device: remote(
+            row_b.at[seat], row_b.at[seat], ag_send.at[1], ag_recv.at[1], device).start())
 
     def group_wait():
         view = row_b.at[pl.ds(0, group - 1)]
@@ -123,15 +146,9 @@
         slot = turn - 1
         row_all[slot, number] = row
 
-        for dz in FAR_FIRST:
-            side = lax.rem(zpos + dz, ZG)
-
-            @pl.loop(0 if dz else 1, group, unroll=8 if dz else 1)
-            def _(step):
-                other = lax.rem(seat + step, group)
-                device = (lax.div(other, xg), lax.rem(other, xg) * ZG + side)
-                remote(row_all.at[slot, number], row_all.at[slot, number], all_sends.at[slot],
-                       all_recvs.at[slot], device).start()
+        all_each(lambda device: remote(
+            row_all.at[slot, number], row_all.at[slot, number], all_sends.at[slot],
+            all_recvs.at[slot], device).start())
 
     def all_wait(turn, what="recv"):
         slot = turn - 1

time: 60.6 us -> 58.8 us (0.970)
  Pallas kernels: 58.1 us -> 56.3 us
    pallas_call x1, Pallas kernels: 58.1 us -> 56.3 us  [local(): pl.pallas_call(body, name='bicgstab', out_shape=jax.ShapeDtypeStruct((2,...]
where the time goes in v6:
time: 58.8 us; the launch traced here: 58.7 us
  Pallas kernels  56.3 us (96%)
  local copies, waits for them, and re-layouts  1.69 us (3%)
  between operations  0.64 us (1%)
    pallas_call x1, Pallas kernels, local(): pl.pallas_call(body, name='bicgstab', out_shape=jax.ShapeDtypeStruct((2,...  56.3 us
    squeeze x1, local copies, waits for them, and re-layouts, local(): return (both[0], both[1])  1.69 us

profile of v6, /device:TPU:1, one launch (start us, length us, event | category | flops | bytes accessed | tf_op | source)
XLA Modules:
  0.0 58.7 jit_solution(14491932706787769138)
XLA Ops:
  0.6 56.3 %bicgstab.1 = f32[2,8,16,256]{3,2,1,0:T(8,128)} custom-call(f32[8,16,256]{2,1,0:T(8,128)} %refs_0_.1, f32[3,8,16,256]{3,2,1,0:T(8,128)} %refs_1_.1, bf16[32,8,16,256]{3,2,1,0:T(8,128)(2,1)} %refs_2_.1, f32[32,8192]{1,0:T(8,128)} %refs_3_.1), custom_call_target="tpu_custom_call" | custom-call | tf_op jit(solution)/shard_map/bicgstab/pallas_call | solution.py:624
  57.0 1.7 %slice_bitcast_fusion = (f32[8,16,256]{2,1,0:T(8,128)}, f32[8,16,256]{2,1,0:T(8,128)}) fusion(f32[2,8,16,256]{3,2,1,0:T(8,128)} %bicgstab.1), kind=kLoop, calls=%fused_computation | loop fusion | bytes 524288 | tf_op jit(solution)/shard_map/squeeze | solution.py:633

commit v7 on v6

--- a/solution.py
+++ b/solution.py
@@ -45,8 +45,8 @@
     r_hbm, vel_hbm, defl_hbm, inv_hbm, both,
     natural, defl, defl_eo, lanes_ref, final, inv, base, base_lo, base_hi, base_plo, base_phi,
     coef, scale, pick, q24, corr, corr_lo, corr_hi, corr_plo, corr_phi, ext, left, upd0, upd1, upd2,
-    face, face_lo, face_hi, face_own, face_plo, face_phi,
-    img, img_lo, img_hi, img_plo, img_phi, search, wfield, s_own, w_own, v_own, row_a, row_b, row_all,
+    face_lo, face_hi, face_plo, face_phi,
+    img, img_lo, img_hi, img_plo, img_phi, search, wfield, v_own, row_a, row_b, row_all,
     local_sem, ag_send, ag_recv, all_sends, all_recvs, halo_send, halo_recv,
 ):
     gx = lax.axis_index("gx")
@@ -82,10 +82,12 @@
         def _(step):
             act((lax.rem(gx + step, ngx), gy))
 
-    def all_each(act):
+    def all_each(act, between=None):
         pairs = [(dz, dx) for dz in range(ZG) for dx in range(xg) if dz or dx]
         pairs.sort(key=lambda p: -hops(p[0], ZG) - hops(p[1], xg))
-        for dz, dx in pairs:
+        for place, (dz, dx) in enumerate(pairs):
+            if place == len(pairs) // 2 and between is not None:
+                between()
             spread(act, dz, dx)
         mine(act)
 
@@ -142,13 +144,13 @@
         view = row_b.at[pl.ds(0, group - 1)]
         remote(view, view, ag_send.at[1], ag_recv.at[1], here).wait_recv()
 
-    def all_send(turn, row):
+    def all_send(turn, row, between=None):
         slot = turn - 1
         row_all[slot, number] = row
 
         all_each(lambda device: remote(
             row_all.at[slot, number], row_all.at[slot, number], all_sends.at[slot],
-            all_recvs.at[slot], device).start())
+            all_recvs.at[slot], device).start(), between)
 
     def all_wait(turn, what="recv"):
         slot = turn - 1
@@ -201,14 +203,15 @@
             else:
                 copy.wait_send()
 
-    def faces(what, slot):
+    def faces(what, slot, field, kinds=(0, 1, 2, 3)):
         pairs = [
-            ((1, 0), face_own.at[slot, 1], face.at[slot, 0]),
-            ((-1, 0), face_own.at[slot, 0], face.at[slot, 1]),
+            ((1, 0), field.at[SX], field.at[0]),
+            ((-1, 0), field.at[1], field.at[SX + 1]),
             ((0, 1), face_phi.at[slot], face_lo.at[slot]),
             ((0, -1), face_plo.at[slot], face_hi.at[slot]),
         ]
-        for k, ((dx, dy), src, dst) in enumerate(pairs):
+        for k in kinds:
+            (dx, dy), src, dst = pairs[k]
             copy = remote(
                 src, dst, halo_send.at[4 + slot, k], halo_recv.at[4 + slot, k],
                 (gx + dx, gy + dy) if what == "start" else here,
@@ -309,7 +312,7 @@
         lhs = jnp.where(iota(shape, 0) == lax.rem(iota(shape, 1), 16), spread, 0.0)
         return split(lhs) if exact else lhs.astype(BF16)
 
-    def smooth(turn, out_ref, own_ref):
+    def smooth(turn, out_ref):
         rows = iota((ROWS, NZ), 0)
         keep_y = ((rows >= 4) & (rows < 20)) | ((rows < 4) & has_s) | ((rows >= 20) & has_n)
         box = (rows >= 2) & (rows < 22)
@@ -358,15 +361,10 @@
             upd3 = factors[2][0] * centre + factors[2][1] * rest
             value = ((upd0[p + 1] + upd1[p]) + (centre + upd3)) + ext[p + 1]
             out_ref[p - 1] = value
-            inner = value[4:20]
-            own_ref[p - 2] = inner
-            face_plo[turn, p - 2] = inner[0:1]
-            face_phi[turn, p - 2] = inner[15:16]
+            face_plo[turn, p - 2] = value[4:5]
+            face_phi[turn, p - 2] = value[19:20]
 
     def face_place(slot, dst):
-        zero4 = jnp.zeros((4, NZ), F32)
-        dst[0] = jnp.where(has_w, jnp.concatenate([zero4, face[slot, 0], zero4], axis=0), 0.0)
-        dst[SX + 1] = jnp.where(has_e, jnp.concatenate([zero4, face[slot, 1], zero4], axis=0), 0.0)
         rows = iota((ROWS, NZ), 0)
 
         @pl.loop(0, SX, unroll=2)
@@ -383,6 +381,13 @@
 
     upd0[0] = jnp.zeros((ROWS, NZ), F32)
     upd0[SX + 5] = jnp.zeros((ROWS, NZ), F32)
+    for there, plane in ((has_w, 0), (has_e, SX + 1)):
+
+        @pl.when(jnp.logical_not(there))
+        def _():
+            search[plane] = jnp.zeros((ROWS, NZ), F32)
+            wfield[plane] = jnp.zeros((ROWS, NZ), F32)
+
     table = lax.div(iota((KD * 16, 128), 0), 16) == lax.rem(iota((KD * 16, 128), 1), KD)
     pick[...] = jnp.where(table, 1.0, 0.0).astype(BF16)
     source, place = iota((NZ, NZ), 0), iota((NZ, NZ), 1)
@@ -454,7 +459,7 @@
 
     loads[4].wait()
 
-    def precondition(turn, out_ref, own_ref, exact):
+    def precondition(turn, out_ref, exact):
         lhs = solve(turn, exact)
         for x in range(SX):
             out = jnp.dot(lhs[:, :256], weights(defl_eo, 0, x), preferred_element_type=F32)
@@ -462,19 +467,18 @@
             if exact:
                 out = out[:16] + out[16:]
             corr[turn, 3 + x] = out
-            corr_plo[turn, x] = out[0:4]
-            corr_phi[turn, x] = out[12:16]
+            corr_plo[turn, x] = out[0:3]
+            corr_phi[turn, x] = out[13:16]
         halo("start", *corr_halo(turn))
         halo("recv", *corr_halo(turn))
-        smooth(turn, out_ref, own_ref)
-        face_own[turn, 0] = own_ref[0]
-        face_own[turn, 1] = own_ref[SX - 1]
-        faces("start", turn)
-        faces("recv", turn)
+        smooth(turn, out_ref)
+        faces("start", turn, out_ref)
+        faces("recv", turn, out_ref)
+        faces("send", turn, out_ref, (0, 1))
         face_place(turn, out_ref)
 
     group_wait()
-    precondition(0, search, s_own, FIRST_EXACT)
+    precondition(0, search, FIRST_EXACT)
 
     @pl.loop(0, SX, unroll=2)
     def _(x):
@@ -484,8 +488,7 @@
         img_phi[x] = inner[14:16]
 
     row = restrict(defl_eo, lambda x: img[DEPTH + x], True)
-    all_send(1, row)
-    halo("start", *img_halo)
+    all_send(1, row, lambda: halo("start", *img_halo))
     halo("recv", *img_halo)
     keep_q = keep_y
 
@@ -494,34 +497,45 @@
         keep = keep_q & ((p >= DEPTH) | has_w) & ((p < SX + DEPTH) | has_e)
         q24[p] = jnp.where(keep, padded(img_lo[p], img[p], img_hi[p]), 0.0)
 
-    all_wait(1)
-    precondition(1, wfield, w_own, True)
-
     zero = jnp.zeros((8, NZ), F32)
 
     def fold(value):
         return value[0:8] + value[8:16]
+
+    def early(x, sums):
+        i = img[DEPTH + x]
+        r = base[3, DEPTH + x]
+        pairs = [(r, r), (r, i), (i, i)]
+        return tuple(s + fold(a * b) for s, (a, b) in zip(sums, pairs))
+
+    early_sums = lax.fori_loop(0, SX, early, (zero,) * 3, unroll=2)
+    lanes = iota((1, 128), 1)
+
+    def pack(row, sums, start):
+        for k, s in enumerate(sums):
+            s = jnp.sum(s, axis=0, keepdims=True)
+            s = jnp.sum(s, axis=1, keepdims=True)
+            row = jnp.where(lanes == start + k, s, row)
+        return row
+
+    early_row = pack(jnp.zeros((1, 128), F32), early_sums, 0)
+    all_wait(1)
+    precondition(1, wfield, True)
 
     def products(x, sums):
         v = operator(x, wfield)[4:20]
         v_own[x] = v
         i = img[DEPTH + x]
         r = base[3, DEPTH + x]
-        pairs = [(r, r), (r, i), (i, i), (v, r), (v, i), (v, v)]
+        pairs = [(v, r), (v, i), (v, v)]
         return tuple(s + fold(a * b) for s, (a, b) in zip(sums, pairs))
 
-    sums = lax.fori_loop(0, SX, products, (zero,) * 6, unroll=2)
-    lanes = iota((1, 128), 1)
-    row = jnp.zeros((1, 128), F32)
-    for k, s in enumerate(sums):
-        s = jnp.sum(s, axis=0, keepdims=True)
-        s = jnp.sum(s, axis=1, keepdims=True)
-        row = jnp.where(lanes == k, s, row)
+    row = pack(early_row, lax.fori_loop(0, SX, products, (zero,) * 3, unroll=2), 3)
     all_send(2, row)
 
     @pl.loop(0, SX)
     def _(x):
-        fields = [s_own[x], img[DEPTH + x], w_own[x], v_own[x]]
+        fields = [search[x + 1][4:20], img[DEPTH + x], wfield[x + 1][4:20], v_own[x]]
         final[:, x] = order(jnp.concatenate(fields, axis=0), True).reshape(4, SY, NZ)
 
     all_wait(2)
@@ -549,7 +563,7 @@
     halo("send", *base_halo)
     for turn in range(2):
         halo("send", *corr_halo(turn))
-        faces("send", turn)
+        faces("send", turn, (search, wfield)[turn], (2, 3))
     halo("send", *img_halo)
 
 
@@ -581,19 +595,17 @@
             vm((KD * 16, 128), BF16),
             vm((SX + 4,) + plane, F32),
             vm((2, SX + 6, SY, NZ), F32),
-            vm((2, SX + 6, 4, NZ), F32),
-            vm((2, SX + 6, 4, NZ), F32),
-            vm((2, SX, 4, NZ), F32),
-            vm((2, SX, 4, NZ), F32),
+            vm((2, SX + 6, 3, NZ), F32),
+            vm((2, SX + 6, 3, NZ), F32),
+            vm((2, SX, 3, NZ), F32),
+            vm((2, SX, 3, NZ), F32),
             vm((SX + 6,) + plane, F32),
             vm((SX + 4,) + plane, F32),
             vm((SX + 6,) + plane, F32),
             vm((SX + 4,) + plane, F32),
             vm((SX + 4,) + plane, F32),
-            vm((2, 2, SY, NZ), F32),
             vm((2, SX, 1, NZ), F32),
             vm((2, SX, 1, NZ), F32),
-            vm((2, 2, SY, NZ), F32),
             vm((2, SX, 1, NZ), F32),
             vm((2, SX, 1, NZ), F32),
             vm((SX + 4, SY, NZ), F32),
@@ -603,8 +615,6 @@
             vm((SX, 2, NZ), F32),
             vm((SX + 2,) + plane, F32),
             vm((SX + 2,) + plane, F32),
-            vm((SX, SY, NZ), F32),
-            vm((SX, SY, NZ), F32),
             vm((SX, SY, NZ), F32),
             vm((ZG, 1, 128), F32),
             vm((group, ZG // QUAD, 128), F32),

time: 58.8 us -> 58.6 us (level)
  no operation moved by 1% of the time
where the time goes in v7:
time: 58.6 us; the launch traced here: 58.5 us
  Pallas kernels  56.2 us (96%)
  local copies, waits for them, and re-layouts  1.69 us (3%)
  between operations  0.64 us (1%)
    pallas_call x1, Pallas kernels, local(): pl.pallas_call(body, name='bicgstab', out_shape=jax.ShapeDtypeStruct((2,...  56.2 us
    squeeze x1, local copies, waits for them, and re-layouts, local(): return (both[0], both[1])  1.69 us

profile of v7, /device:TPU:1, one launch (start us, length us, event | category | flops | bytes accessed | tf_op | source)
XLA Modules:
  0.0 58.5 jit_solution(17242404596043510401)
XLA Ops:
  0.6 56.2 %bicgstab.1 = f32[2,8,16,256]{3,2,1,0:T(8,128)} custom-call(f32[8,16,256]{2,1,0:T(8,128)} %refs_0_.1, f32[3,8,16,256]{3,2,1,0:T(8,128)} %refs_1_.1, bf16[32,8,16,256]{3,2,1,0:T(8,128)(2,1)} %refs_2_.1, f32[32,8192]{1,0:T(8,128)} %refs_3_.1), custom_call_target="tpu_custom_call" | custom-call | tf_op jit(solution)/shard_map/bicgstab/pallas_call | solution.py:634
  56.9 1.7 %slice_bitcast_fusion = (f32[8,16,256]{2,1,0:T(8,128)}, f32[8,16,256]{2,1,0:T(8,128)}) fusion(f32[2,8,16,256]{3,2,1,0:T(8,128)} %bicgstab.1), kind=kLoop, calls=%fused_computation | loop fusion | bytes 524288 | tf_op jit(solution)/shard_map/squeeze | solution.py:643

commit v8 on v7

--- a/solution.py
+++ b/solution.py
@@ -638,7 +638,7 @@
             in_specs=[pl.BlockSpec(memory_space=pl.ANY)] * 4,
             out_specs=pl.BlockSpec(memory_space=vm),
             scratch_shapes=scratch,
-            compiler_params=pltpu.CompilerParams(collective_id=0, has_side_effects=True),
+            compiler_params=pltpu.CompilerParams(collective_id=0, has_side_effects=True, vmem_limit_bytes=56000000),
         )(right_side, velocity, deflation, inverse_rows)
         return both[0], both[1]
 

time: 58.6 us -> 57.8 us (0.986)
  Pallas kernels: 56.2 us -> 55.5 us
    squeeze x1, local copies, waits for them, and re-layouts: 1.69 us -> 0.72 us  [local(): return (both[0], both[1])]
    unnamed x0 -> x2, local copies, waits for them, and re-layouts: none -> 0.9 us
    pallas_call x1, Pallas kernels: 56.2 us -> 55.5 us  [local(): pl.pallas_call(body, name='bicgstab', out_shape=jax.ShapeDtypeStruct((2,...]
where the time goes in v8:
time: 57.8 us; the launch traced here: 57.7 us
  Pallas kernels  55.5 us (96%)
  local copies, waits for them, and re-layouts  1.61 us (3%)
  between operations  0.65 us (1%)
    pallas_call x1, Pallas kernels, local(): pl.pallas_call(body, name='bicgstab', out_shape=jax.ShapeDtypeStruct((2,...  55.5 us

profile of v8, /device:TPU:1, one launch (start us, length us, event | category | flops | bytes accessed | tf_op | source)
XLA Modules:
  0.0 57.7 jit_solution(2682340289248160473)
XLA Ops:
  0.6 0.0 copy-start
  0.6 0.9 %copy-done = f32[8,16,256]{2,1,0:T(8,128)S(1)} copy-done((f32[8,16,256]{2,1,0:T(8,128)S(1)}, f32[8,16,256]{2,1,0:T(8,128)}, u32[]{:S(2)}) %copy-start) | copy-done | bytes 131096
  1.5 55.5 %bicgstab.1 = f32[2,8,16,256]{3,2,1,0:T(8,128)S(1)} custom-call(f32[8,16,256]{2,1,0:T(8,128)S(1)} %copy-done, f32[3,8,16,256]{3,2,1,0:T(8,128)} %refs_1_.1, bf16[32,8,16,256]{3,2,1,0:T(8,128)(2,1)} %refs_2_.1, f32[32,8192]{1,0:T(8,128)} %refs_3_.1), custom_call_target="tpu_custom_call" | custom-call | tf_op jit(solution)/shard_map/bicgstab/pallas_call | solution.py:634
  57.0 0.7 %slice_bitcast_fusion = (f32[8,16,256]{2,1,0:T(8,128)}, f32[8,16,256]{2,1,0:T(8,128)}) fusion(f32[2,8,16,256]{3,2,1,0:T(8,128)S(1)} %bicgstab.1), kind=kLoop, calls=%fused_computation | loop fusion | bytes 524288 | tf_op jit(solution)/shard_map/squeeze | solution.py:643
Async XLA Ops:
  0.6 0.9 %copy-start = (f32[8,16,256]{2,1,0:T(8,128)S(1)}, f32[8,16,256]{2,1,0:T(8,128)}, u32[]{:S(2)}) copy-start(f32[8,16,256]{2,1,0:T(8,128)} %refs_0_.1) | copy-start | bytes 393220
